TPU v7x, 256 devices: a whole 4x4x8 slice. The times are simulated.
256 devices in a mesh: dp: 32 (over x_hi, z, core), tensor: 8 (over y, x_lo).
Axes of the slice: x: 4 (x_hi: 2, x_lo: 2; x = x_hi * 2 + x_lo), y: 4, z: 8, core: 2. Of those that a mesh axis runs over, the one named last changes fastest.
Arguments:
- master: float32 [2, 16384, 16384], P(None, ('tensor', 'dp')), may hold values from -0.1875 to 0.1875
- tile_order: int32 [8, 16], P('tensor'), may hold values from 0 to 15, each once within a row
- check_weights: int32 [8, 16384], P(None, 'tensor'), may hold values from -7 to 7
Outputs:
- tiled: bfloat16 [2, 16384, 16384], P(None, 'tensor', 'dp')
- checksum: float32 [2, 8, 16384], P(None, None, ('dp', 'tensor'))
Inputs may be any that keep to these rules, and one draw needn't show every extreme that they name: Each row of tile_order lists every number of 0 to 15 once.
All inputs are finite; a program needn't handle non-finite values.
Results may differ from a plain program's by a relative error of at most 0.0029.
Values may be sent and summed in bfloat16 or wider, within the bound.
No kernel may reach another device: no remote copies, remote signals or barrier semaphores. Data moves between devices by JAX's collectives and lax.ppermute only.
A program may use at most 128 MiB of HBM per device.

v0:
```python
import jax
import jax.numpy as jnp
from jax import lax
from jax.sharding import PartitionSpec as P

TILE = 128


def on_device(master, tile_order, check_weights):
    tile_rows = TILE
    order = tile_order[0]
    count = order.shape[0]
    low = master.astype(jnp.bfloat16)
    weights = check_weights.astype(jnp.bfloat16)
    received = lax.all_to_all(low, "dp", split_axis=2, concat_axis=1, tiled=True)
    items = received.shape[0]
    columns = received.shape[2]
    blocks = received.reshape(items, count, tile_rows, columns)
    moved = jnp.take(blocks, order, axis=1)
    tiled = moved.reshape(items, count * tile_rows, columns)
    partial_sums = jnp.einsum("cr,lrd->lcd", weights, tiled, preferred_element_type=jnp.float32)
    checksum = lax.psum_scatter(partial_sums, "tensor", scatter_dimension=2, tiled=True)
    return (tiled, checksum)


def solution(mesh):
    in_specs = (P(None, ("tensor", "dp"), None), P("tensor", None), P(None, "tensor"))
    out_specs = (P(None, "tensor", "dp"), P(None, None, ("dp", "tensor")))
    return jax.shard_map(
        on_device, mesh=mesh, in_specs=in_specs, out_specs=out_specs, check_vma=False
    )
```

profile of v0, /device:TPU:4, one launch (start us, length us, event | category | flops | bytes accessed | tf_op | source)
XLA Modules:
  0.0 244.3 jit_solution(6594867219500252485)
XLA Ops:
  7.2 5.9 %convert_element_type.6 = bf16[2,64,16384]{2,1,0:T(8,128)(2,1)} convert(f32[2,64,16384]{2,1,0:T(8,128)} %param.3) | non-fusion elementwise | flops 2097152 | bytes 12582912 | tf_op jit(solution)/shard_map/convert_element_type | solution.py:13
  13.1 17.8 %copy.7 = bf16[2,64,16384]{1,0,2:T(2,128)(2,1)} copy(bf16[2,64,16384]{2,1,0:T(8,128)(2,1)} %convert_element_type.6) | data formatting | bytes 8388608 | tf_op jit(solution)/shard_map/convert_element_type | solution.py:13
  30.9 13.9 %reshape.57 = bf16[32,2,32768]{2,1,0:T(2,128)(2,1)} reshape(bf16[16384,2,64]{2,1,0:T(2,128)(2,1)} %bitcast.26) | data formatting | bytes 8388608
  44.7 0.0 copy-start.2
  44.7 11.8 %all-to-all-start = ((bf16[32,2,32768]{2,1,0:T(2,128)(2,1)}), bf16[32,2,32768]{2,1,0:T(2,128)(2,1)}, u32[]{:S(2)}, u32[]{:S(2)}) async-start(bf16[32,2,32768]{2,1,0:T(2,128)(2,1)} %reshape.57), calls=%async_computation | async-start | bytes 8388608 | tf_op jit(solution)/shard_map/all_to_all | solution.py:15
  56.5 0.0 reduce-scatter.4.cloned.1.call-start
  56.6 0.0 copy-done.2
  56.6 0.1 broadcast_bitcast_fusion
  56.7 93.7 %all-to-all-done = bf16[32,2,32768]{2,1,0:T(2,128)(2,1)} async-done(((bf16[32,2,32768]{2,1,0:T(2,128)(2,1)}), bf16[32,2,32768]{2,1,0:T(2,128)(2,1)}, u32[]{:S(2)}, u32[]{:S(2)}) %all-to-all-start) | async-done | bytes 4194336 | tf_op jit(solution)/shard_map/all_to_all | solution.py:15
  150.3 13.7 %reshape.58 = bf16[16384,2,64]{2,1,0:T(2,128)(2,1)} reshape(bf16[32,2,32768]{2,1,0:T(2,128)(2,1)} %all-to-all-done) | data formatting | bytes 8388608
  164.0 18.5 %copy.12 = bf16[2,64,32,512]{3,1,2,0:T(8,128)(2,1)} copy(bf16[2,64,32,512]{1,0,3,2:T(2,128)(2,1)} %bitcast.27) | data formatting | bytes 8388608 | tf_op jit(solution)/shard_map/all_to_all | solution.py:15
  182.5 4.9 %gather_fusion = bf16[16,2,128,512]{3,2,1,0:T(8,128)(2,1)} fusion(bf16[2,16,128,512]{3,2,1,0:T(8,128)(2,1)} %bitcast.28, s32[1024]{0:T(1024)S(1)} %pad_clamp_fusion), kind=kCustom, calls=%fused_computation | custom fusion | bytes 8388672 | tf_op jit(solution)/shard_map/jit(_take)/gather | solution.py:19
  187.5 2.6 %copy.10 = bf16[2,16,128,512]{3,2,1,0:T(8,128)(2,1)S(1)} copy(bf16[2,16,128,512]{3,2,0,1:T(8,128)(2,1)} %bitcast.29) | data formatting | bytes 8388608 | tf_op jit(solution)/shard_map/jit(_take)/gather | solution.py:19
  190.1 0.0 copy-start.1
  190.1 0.9 bitcast_select_fusion
  191.0 0.0 copy-start
  191.0 2.0 copy-done
  193.0 0.0 copy-done.1
  193.0 0.6 convolution_bitcast_fusion
  193.7 0.3 copy.13
  193.9 1.0 reshape.55
  194.9 0.0 reduce-scatter.4.cloned.1.call-update
  194.9 41.0 %reduce-scatter.4.cloned.1.call-done = f32[64,16]{1,0:T(8,128)} async-done(((f32[512,16]{1,0:T(8,128)}), f32[64,16]{1,0:T(8,128)}) %reduce-scatter.4.cloned.1.call-update) | async-done | bytes 4112
  235.9 0.9 reshape.56
  236.8 0.7 copy.14
  (3 shorter events, 0.0 us)
Async XLA Ops:
  44.7 11.8 %copy-start.2 = (s32[1,16]{1,0:T(1,128)S(1)}, s32[1,16]{1,0:T(1,128)}, u32[]{:S(2)}) copy-start(s32[1,16]{1,0:T(1,128)} %param.4) | copy-start | bytes 196
  44.7 105.6 %all-to-all-start = ((bf16[32,2,32768]{2,1,0:T(2,128)(2,1)}), bf16[32,2,32768]{2,1,0:T(2,128)(2,1)}, u32[]{:S(2)}, u32[]{:S(2)}) async-start(bf16[32,2,32768]{2,1,0:T(2,128)(2,1)} %reshape.57), calls=%async_computation | async-start | bytes 8388608 | tf_op jit(solution)/shard_map/all_to_all | solution.py:15
  56.5 179.4 %reduce-scatter.4.cloned.1.call-start = ((), (), s32[]{:S(2)}) async-start(), calls=%async_computation.2 | async-start | bytes 294912
  190.1 2.9 %copy-start.1 = (s32[8,2048]{1,0:T(8,128)S(1)}, s32[8,2048]{1,0:T(8,128)}, u32[]{:S(2)}) copy-start(s32[8,2048]{1,0:T(8,128)} %param.5) | copy-start | bytes 196612
  191.0 2.0 copy-start
Sparse Core Ops, SparseCore 0:
  195.1 40.8 reduce-scatter.3
where the time goes:
time: 246 us; the launch traced here: 244 us
  waiting for transfers between devices  135 us (55%)
  local copies, waits for them, and re-layouts  76.3 us (31%)
  between operations  14.1 us (6%)
  starting transfers between devices  11.8 us (5%)
  other arithmetic  6.79 us (3%)
    all_to_all x1, waiting for transfers between devices, on_device(): lax.all_to_all(low, 'dp', split_axis=2, concat_axis=1, tiled=True)  93.7 us
    unnamed x2, waiting for transfers between devices  41 us
    unnamed x12, local copies, waits for them, and re-layouts  32.3 us
    all_to_all x1, local copies, waits for them, and re-layouts, on_device(): lax.all_to_all(low, 'dp', split_axis=2, concat_axis=1, tiled=True)  18.5 us
    convert_element_type x1, local copies, waits for them, and re-layouts, on_device(): low = master.astype(jnp.bfloat16)  17.8 us
    all_to_all x1, starting transfers between devices, on_device(): lax.all_to_all(low, 'dp', split_axis=2, concat_axis=1, tiled=True)  11.8 us
    gather x2, local copies, waits for them, and re-layouts, on_device(): moved = jnp.take(blocks, order, axis=1)  7.57 us
    convert_element_type x1, other arithmetic, on_device(): low = master.astype(jnp.bfloat16)  5.9 us
  transfers between devices with their start and end apart: 2, of which 2 were waited for; matrix products, arithmetic and copies ran while one was open for 0% of the time, Pallas kernels for 0%

commit v1 on v0

v1 whole, which is shorter than its diff:
```python
import functools

import jax
import jax.numpy as jnp
from jax import lax
from jax.experimental import pallas as pl
from jax.experimental.pallas import tpu as pltpu
from jax.sharding import PartitionSpec as P

TILE = 128


def pack_kernel(master_ref, out_ref):
    per_step, layers, rows, columns = out_ref.shape
    for i in range(per_step):
        for l in range(layers):
            block = master_ref[l, :, i * columns:(i + 1) * columns]
            out_ref[i, l] = block.astype(jnp.bfloat16)


def pack(master, parts, per_step):
    layers, rows, width = master.shape
    columns = width // parts
    return pl.pallas_call(
        pack_kernel,
        grid=(parts // per_step,),
        in_specs=[pl.BlockSpec((layers, rows, per_step * columns), lambda i: (0, 0, i))],
        out_specs=pl.BlockSpec((per_step, layers, rows, columns), lambda i: (i, 0, 0, 0)),
        out_shape=jax.ShapeDtypeStruct((parts, layers, rows, columns), jnp.bfloat16),
        name="pack",
    )(master)


def regroup_kernel(order_ref, weights_ref, received_ref, tiled_ref, sums_ref, held, in_sems, out_sems):
    count = in_sems.shape[0]
    parts, layers, rows, columns = held.shape
    halves = parts // count
    groups, _, width = sums_ref.shape

    def fetch(k):
        source = order_ref[k]
        return pltpu.make_async_copy(
            received_ref.at[pl.ds(source * halves, halves)],
            held.at[pl.ds(k * halves, halves)],
            in_sems.at[k],
        )

    def put(k, h, l):
        part = k * halves + h
        return pltpu.make_async_copy(
            held.at[part, l],
            tiled_ref.at[l, pl.ds(part * rows, rows)],
            out_sems.at[k, h, l],
        )

    for k in range(count):
        fetch(k).start()
    sums = [jnp.zeros((weights_ref.shape[0], columns), jnp.float32) for _ in range(layers)]
    for k in range(count):
        fetch(k).wait()
        for h in range(halves):
            for l in range(layers):
                put(k, h, l).start()
        for h in range(halves):
            part = k * halves + h
            weights = weights_ref[:, part * rows:(part + 1) * rows].astype(jnp.float32).astype(jnp.bfloat16)
            for l in range(layers):
                sums[l] += jnp.dot(weights, held[part, l], preferred_element_type=jnp.float32)
    each = width // layers
    for t in range(groups):
        pieces = [sums[l][:, t * each:(t + 1) * each] for l in range(layers)]
        sums_ref[t] = jnp.concatenate(pieces, axis=1)
    for k in range(count):
        for h in range(halves):
            for l in range(layers):
                put(k, h, l).wait()


def regroup(order, weights, received, groups):
    parts, layers, rows, columns = received.shape
    count = order.shape[0]
    halves = parts // count
    checks = weights.shape[0]
    return pl.pallas_call(
        regroup_kernel,
        in_specs=[
            pl.BlockSpec(memory_space=pltpu.SMEM),
            pl.BlockSpec(memory_space=pltpu.VMEM),
            pl.BlockSpec(memory_space=pl.ANY),
        ],
        out_specs=[
            pl.BlockSpec(memory_space=pl.ANY),
            pl.BlockSpec(memory_space=pltpu.VMEM),
        ],
        out_shape=[
            jax.ShapeDtypeStruct((layers, parts * rows, columns), jnp.bfloat16),
            jax.ShapeDtypeStruct((groups, checks, layers * columns // groups), jnp.float32),
        ],
        scratch_shapes=[
            pltpu.VMEM((parts, layers, rows, columns), jnp.bfloat16),
            pltpu.SemaphoreType.DMA((count,)),
            pltpu.SemaphoreType.DMA((count, halves, layers)),
        ],
        name="regroup",
    )(order, weights, received)


def total_kernel(parts_ref, out_ref):
    total = parts_ref[0]
    for t in range(1, parts_ref.shape[0]):
        total += parts_ref[t]
    layers, _, each = out_ref.shape
    for l in range(layers):
        out_ref[l] = total[:, l * each:(l + 1) * each]


def on_device(parts, groups, master, tile_order, check_weights):
    layers = master.shape[0]
    packed = pack(master, parts, 4)
    received = lax.all_to_all(packed, "dp", split_axis=0, concat_axis=0, tiled=True)
    tiled, sums = regroup(tile_order[0], check_weights, received, groups)
    sums = lax.all_to_all(sums, "tensor", split_axis=0, concat_axis=0, tiled=True)
    checks, width = sums.shape[1:]
    checksum = pl.pallas_call(
        total_kernel,
        out_shape=jax.ShapeDtypeStruct((layers, checks, width // layers), jnp.float32),
        name="total",
    )(sums)
    return (tiled, checksum)


def solution(mesh):
    in_specs = (P(None, ("tensor", "dp"), None), P("tensor", None), P(None, "tensor"))
    out_specs = (P(None, "tensor", "dp"), P(None, None, ("dp", "tensor")))
    body = functools.partial(on_device, mesh.shape["dp"], mesh.shape["tensor"])
    return jax.shard_map(body, mesh=mesh, in_specs=in_specs, out_specs=out_specs, check_vma=False)
```

time: 246 us -> 136 us (0.55)
  waiting for transfers between devices: 135 us -> 0 us
  blocking collectives: 0 us -> 118 us
  local copies, waits for them, and re-layouts: 76.3 us -> 0 us
  Pallas kernels: 0 us -> 14.9 us
  between operations: 14.1 us -> 0.64 us
  starting transfers between devices: 11.8 us -> 0 us
  other arithmetic: 6.79 us -> 0 us
    all_to_all x0 -> x2, blocking collectives: none -> 118 us  [the longest x1 106 us: on_device(): lax.all_to_all(packed, 'dp', split_axis=0, concat_axis=0, tiled=True)]
    all_to_all x1 -> x0, waiting for transfers between devices: 93.7 us -> none  [on_device(): lax.all_to_all(low, 'dp', split_axis=2, concat_axis=1, tiled=True)]
    unnamed x2 -> x0, waiting for transfers between devices: 41 us -> none
    unnamed x12 -> x0, local copies, waits for them, and re-layouts: 32.3 us -> none
    all_to_all x1 -> x0, local copies, waits for them, and re-layouts: 18.5 us -> none  [on_device(): lax.all_to_all(low, 'dp', split_axis=2, concat_axis=1, tiled=True)]
    convert_element_type x1 -> x0, local copies, waits for them, and re-layouts: 17.8 us -> none  [on_device(): low = master.astype(jnp.bfloat16)]
    pallas_call x0 -> x3, Pallas kernels: none -> 14.9 us  [the longest x1 7.69 us: pack(): pl.pallas_call(pack_kernel, grid=(parts // per_step,), in_specs=[pl.Block...]
    all_to_all x1 -> x0, starting transfers between devices: 11.8 us -> none  [on_device(): lax.all_to_all(low, 'dp', split_axis=2, concat_axis=1, tiled=True)]
  transfers between devices with their start and end apart: 2 -> 0, of which waited for: 2 -> 0; matrix products, arithmetic and copies ran while one was open for 0% -> 0% of each run, Pallas kernels for 0% -> 0%
where the time goes in v1:
time: 136 us; the launch traced here: 133 us
  blocking collectives  118 us (87%)
  Pallas kernels  14.9 us (11%)
    all_to_all x1, blocking collectives, on_device(): lax.all_to_all(packed, 'dp', split_axis=0, concat_axis=0, tiled=True)  106 us
    all_to_all x1, blocking collectives, on_device(): lax.all_to_all(sums, 'tensor', split_axis=0, concat_axis=0, tiled=True)  11.5 us
    pallas_call x1, Pallas kernels, pack(): pl.pallas_call(pack_kernel, grid=(parts // per_step,), in_specs=[pl.Block...  7.69 us
    pallas_call x1, Pallas kernels, regroup(): pl.pallas_call(regroup_kernel, in_specs=[pl.BlockSpec(memory_space=pltpu....  5.77 us

profile of v1, /device:TPU:4, one launch (start us, length us, event | category | flops | bytes accessed | tf_op | source)
XLA Modules:
  0.0 133.5 jit_solution(7236855706778167786)
XLA Ops:
  0.6 7.7 %pack.1 = bf16[32,2,64,512]{3,2,1,0:T(8,128)(2,1)} custom-call(f32[2,64,16384]{2,1,0:T(8,128)} %master_ref.1), custom_call_target="tpu_custom_call" | custom-call | tf_op jit(solution)/shard_map/pack/pallas_call | solution.py:24
  8.3 106.5 %all_to_all.10.received_ref = bf16[32,2,64,512]{3,2,1,0:T(8,128)(2,1)} all-to-all(bf16[32,2,64,512]{3,2,1,0:T(8,128)(2,1)} %pack.1), channel_id=1, replica_groups=mesh['dp'=32,'tensor'=8] {'dp'}, dimensions={0} | all-to-all | bytes 8388608 | tf_op jit(solution)/shard_map/all_to_all | solution.py:120
  114.8 5.8 %regroup.1 = (bf16[2,2048,512]{2,1,0:T(8,128)(2,1)}, f32[8,8,128]{2,1,0:T(8,128)}) custom-call(s32[16]{0:T(128)} %bitcast.1, s32[8,2048]{1,0:T(8,128)} %weights_ref.1, bf16[32,2,64,512]{3,2,1,0:T(8,128)(2,1)} %all_to_all.10.received_ref), custom_call_target="tpu_custom_call" | custom-call | tf_op jit(solution)/shard_map/regroup/pallas_call | solution.py:84
  120.6 11.5 %all_to_all.11.parts_ref = f32[8,8,128]{2,1,0:T(8,128)} all-to-all(f32[8,8,128]{2,1,0:T(8,128)} %get-tuple-element.5), channel_id=1, replica_groups=mesh['dp'=32,'tensor'=8] {'tensor'}, dimensions={0} | all-to-all | bytes 65536 | tf_op jit(solution)/shard_map/all_to_all | solution.py:122
  132.1 1.4 %total.1 = f32[2,8,64]{2,1,0:T(8,128)} custom-call(f32[8,8,128]{2,1,0:T(8,128)} %all_to_all.11.parts_ref), custom_call_target="tpu_custom_call" | custom-call | tf_op jit(solution)/shard_map/total/pallas_call | solution.py:124

commit v2 on v0

v2 whole, which is shorter than its diff:
```python
import functools

import jax
import jax.numpy as jnp
from jax import lax
from jax.experimental import pallas as pl
from jax.experimental.pallas import tpu as pltpu
from jax.sharding import PartitionSpec as P


NX, NZ = 2, 8
DIRECT = ((0, 4), (1, 4))
FIRST = ((1, 3), (1, 5), (0, 3), (0, 5))
SECOND = ((1, 2), (1, 6), (0, 2), (0, 6), (1, 0))
THIRD = ((1, 1), (1, 7), (0, 1), (0, 7))
SWAPPED = FIRST + SECOND + THIRD


GRANT = 12 * 2**20
PACK_GRANT = 56 * 2**20


def send(array, delta):
    return lax.ppermute(array, "dp", shift(*delta))


def position():
    me = lax.axis_index("dp")
    core = lax.rem(me, 2)
    chip = me // 2
    return chip // NZ, lax.rem(chip, NZ), core


def device_at(dx, dz, dc):
    x, z, core = position()
    return (lax.rem(x + dx, NX) * NZ + lax.rem(z + dz, NZ)) * 2 + lax.rem(core + dc, 2)


def shift(dx, dz, dc):
    pairs = []
    for x in range(NX):
        for z in range(NZ):
            for core in range(2):
                target = ((x + dx) % NX * NZ + (z + dz) % NZ) * 2 + (core + dc) % 2
                pairs.append(((x * NZ + z) * 2 + core, target))
    return pairs


def pack_kernel(blocks, copies, *refs):
    n_out = 1 + max(out for _, out, _ in blocks)
    master_ref = refs[0]
    swapped_ref = refs[1] if copies else None
    first = 2 if copies else 1
    outs = refs[first:first + n_out]
    wide, low, in_sems, out_sems = refs[first + n_out:]
    layers, _, columns = wide.shape[1:]

    def fetch(i):
        start = pl.multiple_of(device_at(*blocks[i][0]) * columns, columns)
        return pltpu.make_async_copy(master_ref.at[:, :, pl.ds(start, columns)], wide.at[i], in_sems.at[i])

    def fetch_copy(i):
        j = len(blocks) + i
        return pltpu.make_async_copy(swapped_ref.at[copies[i][0]], low.at[j], in_sems.at[j])

    def put(j, out, slot):
        target = outs[out] if slot is None else outs[out].at[slot]
        return pltpu.make_async_copy(low.at[j], target, out_sems.at[j])

    for i in range(len(blocks)):
        fetch(i).start()
    for i in range(len(copies)):
        fetch_copy(i).start()
    for i in range(len(blocks)):
        fetch(i).wait()
        for l in range(layers):
            low[i, l] = wide[i, l].astype(jnp.bfloat16)
        put(i, blocks[i][1], blocks[i][2]).start()
    for i in range(len(copies)):
        fetch_copy(i).wait()
        put(len(blocks) + i, copies[i][1], copies[i][2]).start()
    for i in range(len(blocks)):
        put(i, blocks[i][1], blocks[i][2]).wait()
    for i in range(len(copies)):
        put(len(blocks) + i, copies[i][1], copies[i][2]).wait()


def pack(master, swapped, parts, blocks, copies, shapes):
    layers, rows, width = master.shape
    columns = width // parts
    count = len(blocks) + len(copies)
    operands = (master, swapped) if copies else (master,)
    piece = layers * rows * columns * 2
    return pl.pallas_call(
        functools.partial(pack_kernel, blocks, copies),
        in_specs=[pl.BlockSpec(memory_space=pltpu.HBM)] + [pl.BlockSpec(memory_space=pl.ANY)] * (len(operands) - 1),
        out_specs=[pl.BlockSpec(memory_space=pl.ANY)] * len(shapes),
        out_shape=[jax.ShapeDtypeStruct(s + (layers, rows, columns), jnp.bfloat16) for s in shapes],
        scratch_shapes=[
            pltpu.VMEM((len(blocks), layers, rows, columns), jnp.float32),
            pltpu.VMEM((count, layers, rows, columns), jnp.bfloat16),
            pltpu.SemaphoreType.DMA((count,)),
            pltpu.SemaphoreType.DMA((count,)),
        ],
        cost_estimate=pl.CostEstimate(
            flops=0, transcendentals=0, bytes_accessed=piece * (3 * len(blocks) + 2 * len(copies))
        ),
        compiler_params=pltpu.CompilerParams(vmem_limit_bytes=PACK_GRANT if not copies else GRANT),
    )(*operands)


def regroup_kernel(chips, aliased, groups, *refs):
    order_ref, weights_ref = refs[:2]
    n_in = sum(2 if split else 1 for _, split in chips)
    pieces = refs[2:2 + n_in]
    rest = refs[2 + n_in:]
    sums_in = None
    if aliased:
        sums_in, rest = rest[0], rest[2:]
    tiled_ref, sums_ref, place, held, in_sems, out_sems = rest
    count = order_ref.shape[0]
    layers, tile_rows, columns = held.shape[1:]
    rows = tile_rows // 2
    x, z, core = position()

    for k in range(count):
        place[order_ref[k]] = k

    where = []
    for dx, dz in [delta for delta, _ in chips]:
        chip = lax.rem(x + NX - dx, NX) * NZ + lax.rem(z + NZ - dz, NZ)
        where.append(place[chip])

    copies = []
    at = 0
    for i, (_, split) in enumerate(chips):
        for slot in range(2):
            source = pieces[at + slot] if split else pieces[at].at[slot]
            half = core if slot == 0 else 1 - core
            start = pl.multiple_of(half * rows, rows)
            copies.append(pltpu.make_async_copy(source, held.at[i, :, pl.ds(start, rows)], in_sems.at[i, slot]))
        at += 2 if split else 1

    def put(i, l):
        start = pl.multiple_of(where[i] * tile_rows, tile_rows)
        return pltpu.make_async_copy(held.at[i, l], tiled_ref.at[l, pl.ds(start, tile_rows)], out_sems.at[i, l])

    for copy in copies:
        copy.start()
    checks = weights_ref.shape[0]
    sums = [sums_in[l] if aliased else jnp.zeros((checks, columns), jnp.float32) for l in range(layers)]
    for i in range(len(chips)):
        copies[2 * i].wait()
        copies[2 * i + 1].wait()
        for l in range(layers):
            put(i, l).start()
        start = pl.multiple_of(where[i] * tile_rows, tile_rows)
        weights = weights_ref[:, pl.ds(start, tile_rows)].astype(jnp.float32).astype(jnp.bfloat16)
        for l in range(layers):
            sums[l] += jnp.dot(weights, held[i, l], preferred_element_type=jnp.float32)
    if groups:
        each = columns // groups
        for t in range(groups):
            sums_ref[t] = jnp.concatenate([s[:, t * each:(t + 1) * each] for s in sums], axis=1)
    else:
        for l in range(layers):
            sums_ref[l] = sums[l]
    for i in range(len(chips)):
        for l in range(layers):
            put(i, l).wait()


def regroup(order, weights, pieces, chips, before, groups):
    layers, rows, columns = pieces[0].shape[-3:]
    count = order.shape[0]
    checks, height = weights.shape
    any_space = pl.BlockSpec(memory_space=pl.ANY)
    vmem = pl.BlockSpec(memory_space=pltpu.VMEM)
    specs = [pl.BlockSpec(memory_space=pltpu.SMEM), vmem] + [any_space] * len(pieces)
    operands = [order, weights, *pieces]
    aliases = {}
    if before is not None:
        tiled, sums = before
        operands += [sums, tiled]
        specs += [vmem, pl.BlockSpec(memory_space=pltpu.HBM)]
        aliases = {len(operands) - 1: 0}
    shape = (groups, checks, layers * columns // groups) if groups else (layers, checks, columns)
    n = len(chips)
    hbm = pl.BlockSpec(memory_space=pltpu.HBM)
    return pl.pallas_call(
        functools.partial(regroup_kernel, chips, before is not None, groups),
        in_specs=specs,
        out_specs=[hbm, vmem],
        out_shape=[
            jax.ShapeDtypeStruct((layers, height, columns), jnp.bfloat16),
            jax.ShapeDtypeStruct(shape, jnp.float32),
        ],
        scratch_shapes=[
            pltpu.SMEM((count,), jnp.int32),
            pltpu.VMEM((n, layers, 2 * rows, columns), jnp.bfloat16),
            pltpu.SemaphoreType.DMA((n, 2)),
            pltpu.SemaphoreType.DMA((n, layers)),
        ],
        input_output_aliases=aliases,
        cost_estimate=pl.CostEstimate(
            flops=2 * n * checks * layers * 2 * rows * columns,
            transcendentals=0,
            bytes_accessed=2 * n * layers * 2 * rows * columns * 2,
        ),
        compiler_params=pltpu.CompilerParams(vmem_limit_bytes=GRANT),
    )(*operands)


def total_kernel(parts_ref, out_ref):
    total = parts_ref[0]
    for t in range(1, parts_ref.shape[0]):
        total += parts_ref[t]
    layers, _, each = out_ref.shape
    for l in range(layers):
        out_ref[l] = total[:, l * each:(l + 1) * each]


def on_device(parts, groups, master, tile_order, check_weights):
    layers = master.shape[0]
    order = tile_order[0]

    blocks = tuple((delta + (dc,), 2 * i + dc, None) for i, delta in enumerate(DIRECT) for dc in range(2))
    direct = pack(master, None, parts, blocks, (), [()] * len(blocks))
    direct = [send(a, b[0]) for a, b in zip(direct, blocks)]

    mine = ((0, 0),) + SWAPPED
    blocks = tuple((delta + (1,), 0, i) for i, delta in enumerate(mine))
    (sibling,) = pack(master, None, parts, blocks, (), [(len(mine),)])
    swapped = send(sibling, (0, 0, 1))

    blocks = tuple((delta + (0,), i, 0) for i, delta in enumerate(mine))
    copies = tuple((i, i, 1) for i in range(len(mine)))
    pieces = pack(master, swapped, parts, blocks, copies, [(2,)] * len(mine))
    here, pieces = pieces[0], pieces[1:]
    moved = {d: send(a, d + (0,)) for d, a in zip(SWAPPED, pieces)}

    chips = (((0, 0), False),) + tuple((d, True) for d in DIRECT) + tuple((d, False) for d in FIRST)
    state = regroup(order, check_weights, [here, *direct, *(moved[d] for d in FIRST)], chips, None, 0)
    chips = tuple((d, False) for d in SECOND)
    state = regroup(order, check_weights, [moved[d] for d in SECOND], chips, state, 0)
    chips = tuple((d, False) for d in THIRD)
    tiled, sums = regroup(order, check_weights, [moved[d] for d in THIRD], chips, state, groups)

    sums = lax.all_to_all(sums, "tensor", split_axis=0, concat_axis=0, tiled=True)
    checks, width = sums.shape[1:]
    checksum = pl.pallas_call(
        total_kernel,
        out_shape=jax.ShapeDtypeStruct((layers, checks, width // layers), jnp.float32),
        name="total",
    )(sums)
    return (tiled, checksum)


def solution(mesh):
    in_specs = (P(None, ("tensor", "dp"), None), P("tensor", None), P(None, "tensor"))
    out_specs = (P(None, "tensor", "dp"), P(None, None, ("dp", "tensor")))

    def body(*args):
        return on_device(mesh.shape["dp"], mesh.shape["tensor"], *args)

    return jax.shard_map(body, mesh=mesh, in_specs=in_specs, out_specs=out_specs, check_vma=False)
```

time: 246 us -> 139 us (0.57)
  waiting for transfers between devices: 135 us -> 39.4 us
  local copies, waits for them, and re-layouts: 76.3 us -> 3.4 us
  starting transfers between devices: 11.8 us -> 60.1 us
  Pallas kernels: 0 us -> 23.5 us
  between operations: 14.1 us -> 0.73 us
  blocking collectives: 0 us -> 11.5 us
  other arithmetic: 6.79 us -> 0 us
    all_to_all x1 -> x0, waiting for transfers between devices: 93.7 us -> none  [on_device(): lax.all_to_all(low, 'dp', split_axis=2, concat_axis=1, tiled=True)]
    ppermute x0 -> x18, starting transfers between devices: none -> 60.1 us  [send(): return lax.ppermute(array, 'dp', shift(*delta))]
    unnamed x2 -> x0, waiting for transfers between devices: 41 us -> none
    ppermute x0 -> x18, waiting for transfers between devices: none -> 39.4 us  [send(): return lax.ppermute(array, 'dp', shift(*delta))]
    unnamed x12 -> x10, local copies, waits for them, and re-layouts: 32.3 us -> 3.4 us
    pallas_call x0 -> x7, Pallas kernels: none -> 23.5 us  [the longest x3 13.8 us: pack(): pl.pallas_call(functools.partial(pack_kernel, blocks, copies), in_specs=[...]
    all_to_all x1 -> x0, local copies, waits for them, and re-layouts: 18.5 us -> none  [on_device(): lax.all_to_all(low, 'dp', split_axis=2, concat_axis=1, tiled=True)]
    convert_element_type x1 -> x0, local copies, waits for them, and re-layouts: 17.8 us -> none  [on_device(): low = master.astype(jnp.bfloat16)]
  transfers between devices with their start and end apart: 2 -> 18, of which waited for: 2 -> 7; matrix products, arithmetic and copies ran while one was open for 0% -> 0% of each run, Pallas kernels for 0% -> 12%
where the time goes in v2:
time: 139 us
  starting transfers between devices  60.1 us (43%)
  waiting for transfers between devices  39.4 us (28%)
  Pallas kernels  23.5 us (17%)
  blocking collectives  11.5 us (8%)
  local copies, waits for them, and re-layouts  3.4 us (2%)
    ppermute x18, starting transfers between devices, send(): return lax.ppermute(array, 'dp', shift(*delta))  60.1 us
    ppermute x18, waiting for transfers between devices, send(): return lax.ppermute(array, 'dp', shift(*delta))  39.4 us
    pallas_call x3, Pallas kernels, pack(): pl.pallas_call(functools.partial(pack_kernel, blocks, copies), in_specs=[...  13.8 us
    all_to_all x1, blocking collectives, on_device(): lax.all_to_all(sums, 'tensor', split_axis=0, concat_axis=0, tiled=True)  11.5 us
    pallas_call x3, Pallas kernels, regroup(): pl.pallas_call(functools.partial(regroup_kernel, chips, before is not Non...  8.26 us
    unnamed x10, local copies, waits for them, and re-layouts  3.4 us
  transfers between devices with their start and end apart: 18, of which 7 were waited for; matrix products, arithmetic and copies ran while one was open for 0% of the time, Pallas kernels for 12%

profile of v2, /device:TPU:4, one launch (start us, length us, event | category | flops | bytes accessed | tf_op | source)
XLA Modules:
  0.0 138.6 jit_solution(7604527040766269603)
XLA Ops:
  0.6 3.1 %shard_map.50 = bf16[14,2,64,512]{3,2,1,0:T(8,128)(2,1)} custom-call(f32[2,64,16384]{2,1,0:T(8,128)} %refs_0_.5), custom_call_target="tpu_custom_call" | custom-call | bytes 5505024 | tf_op jit(solution)/shard_map/pallas_call | solution.py:94
  3.8 0.1 collective-permute-start
  3.9 1.9 %shard_map.52 = (bf16[2,64,512]{2,1,0:T(8,128)(2,1)}, bf16[2,64,512]{2,1,0:T(8,128)(2,1)}, bf16[2,64,512]{2,1,0:T(8,128)(2,1)}, bf16[2,64,512]{2,1,0:T(8,128)(2,1)}) custom-call(f32[2,64,16384]{2,1,0:T(8,128)} %refs_0_.5), custom_call_target="tpu_custom_call" | custom-call | bytes 1572864 | tf_op jit(solution)/shard_map/pallas_call | solution.py:94
  5.8 7.3 %collective-permute-start.10 = (bf16[2,64,512]{2,1,0:T(8,128)(2,1)}, bf16[2,64,512]{2,1,0:T(8,128)(2,1)S(1)}, u32[]{:S(2)}, u32[]{:S(2)}) collective-permute-start(bf16[2,64,512]{2,1,0:T(8,128)(2,1)} %get-tuple-element.36), channel_id=1, source_target_pairs={{0,64},{8,72},{16,80},{24,88},{32,96},{40,104},{48,112},{56,120},{... | collective-permute-start | bytes 393224 | tf_op jit(solution)/shard_map/ppermute | solution.py:24
  13.1 0.0 copy-start.2
  13.1 0.2 collective-permute-start.11
  13.3 0.0 collective-permute-done.refs_1_
  13.3 0.0 copy-start
  13.3 3.4 %copy-done = f32[2,64,16384]{2,1,0:T(8,128)S(1)} copy-done((f32[2,64,16384]{2,1,0:T(8,128)S(1)}, f32[2,64,16384]{2,1,0:T(8,128)}, u32[]{:S(2)}) %copy-start) | copy-done | bytes 8388632
  16.7 0.0 copy-start.4
  16.7 0.0 copy-start.3
  16.7 0.0 copy-start.1
  16.7 8.7 %shard_map.51 = (bf16[2,2,64,512]{3,2,1,0:T(8,128)(2,1)S(1)}, bf16[2,2,64,512]{3,2,1,0:T(8,128)(2,1)S(1)}, bf16[2,2,64,512]{3,2,1,0:T(8,128)(2,1)S(1)}, bf16[2,2...) custom-call(f32[2,64,16384]{2,1,0:T(8,128)S(1)} %copy-done, ...), custom_call_target="tpu_custom_call" | custom-call | bytes 9175040 | tf_op jit(solution)/shard_map/pallas_call | solution.py:94
  25.4 1.6 %collective-permute-start.5 = (bf16[2,2,64,512]{3,2,1,0:T(8,128)(2,1)S(1)}, bf16[2,2,64,512]{3,2,1,0:T(8,128)(2,1)S(1)}, u32[]{:S(2)}, u32[]{:S(2)}) collective-permute-start(bf16[2,2,64,512]{3,2,1,0:T(8,128)(2,1)S(1)} %get-tuple-element.30), channel_id=1, source_target_pairs={{0,160},{8,168},{16,176},{24,184},{32,192},{40,200},{48,208},{56,2... | collective-permute-start | bytes 786440 | tf_op jit(solution)/shard_map/ppermute | solution.py:24
  27.0 5.0 %collective-permute-start.6 = (bf16[2,2,64,512]{3,2,1,0:T(8,128)(2,1)S(1)}, bf16[2,2,64,512]{3,2,1,0:T(8,128)(2,1)S(1)}, u32[]{:S(2)}, u32[]{:S(2)}) collective-permute-start(bf16[2,2,64,512]{3,2,1,0:T(8,128)(2,1)S(1)} %get-tuple-element.31), channel_id=1, source_target_pairs={{0,224},{8,232},{16,240},{24,248},{32,128},{40,136},{48,144},{56,1... | collective-permute-start | bytes 786440 | tf_op jit(solution)/shard_map/ppermute | solution.py:24
  32.0 0.4 collective-permute-start.7
  32.4 0.0 collective-permute-done.10.refs_3_
  32.4 0.0 copy-done.4
  32.4 5.3 %collective-permute-start.12 = (bf16[2,64,512]{2,1,0:T(8,128)(2,1)S(1)}, bf16[2,64,512]{2,1,0:T(8,128)(2,1)S(1)}, u32[]{:S(2)}, u32[]{:S(2)}) collective-permute-start(bf16[2,64,512]{2,1,0:T(8,128)(2,1)S(1)} %copy-done.4), channel_id=1, source_target_pairs={{0,192},{8,200},{16,208},{24,216},{32,224},{40,232},{48,240},{56,2... | collective-permute-start | bytes 393224 | tf_op jit(solution)/shard_map/ppermute | solution.py:24
  37.8 0.0 collective-permute-done.11.refs_4_
  37.8 0.0 copy-done.3
  37.8 1.8 %collective-permute-start.13 = (bf16[2,64,512]{2,1,0:T(8,128)(2,1)S(1)}, bf16[2,64,512]{2,1,0:T(8,128)(2,1)S(1)}, u32[]{:S(2)}, u32[]{:S(2)}) collective-permute-start(bf16[2,64,512]{2,1,0:T(8,128)(2,1)S(1)} %copy-done.3), channel_id=1, source_target_pairs={{0,200},{8,192},{16,216},{24,208},{32,232},{40,224},{48,248},{56,2... | collective-permute-start | bytes 393224 | tf_op jit(solution)/shard_map/ppermute | solution.py:24
  39.6 16.2 %collective-permute-done.12.refs_5_ = bf16[2,64,512]{2,1,0:T(8,128)(2,1)S(1)} collective-permute-done((bf16[2,64,512]{2,1,0:T(8,128)(2,1)S(1)}, bf16[2,64,512]{2,1,0:T(8,128)(2,1)S(1)}, u32[]{:S(2)}, u32[]{:S(2)}) %collective-permute-start.12) | collective-permute-done | bytes 131104 | tf_op jit(solution)/shard_map/ppermute | solution.py:24
  55.8 10.0 %collective-permute-start.8 = (bf16[2,2,64,512]{3,2,1,0:T(8,128)(2,1)S(1)}, bf16[2,2,64,512]{3,2,1,0:T(8,128)(2,1)S(1)}, u32[]{:S(2)}, u32[]{:S(2)}) collective-permute-start(bf16[2,2,64,512]{3,2,1,0:T(8,128)(2,1)S(1)} %get-tuple-element.33), channel_id=1, source_target_pairs={{0,96},{8,104},{16,112},{24,120},{32,0},{40,8},{48,16},{56,24},{64... | collective-permute-start | bytes 786440 | tf_op jit(solution)/shard_map/ppermute | solution.py:24
  65.8 0.0 collective-permute-done.13.refs_6_
  65.8 0.0 collective-permute-start.14
  65.8 0.0 collective-permute-done.5.refs_2_
  65.8 7.4 %collective-permute-start.15 = (bf16[2,2,64,512]{3,2,1,0:T(8,128)(2,1)S(1)}, bf16[2,2,64,512]{3,2,1,0:T(8,128)(2,1)S(1)}, u32[]{:S(2)}, u32[]{:S(2)}) collective-permute-start(bf16[2,2,64,512]{3,2,1,0:T(8,128)(2,1)S(1)} %get-tuple-element.41), channel_id=1, source_target_pairs={{0,208},{8,216},{16,224},{24,232},{32,240},{40,248},{48,128},{56,1... | collective-permute-start | bytes 786440 | tf_op jit(solution)/shard_map/ppermute | solution.py:24
  73.2 0.0 collective-permute-done.6.refs_3_
  73.2 0.8 collective-permute-start.16
  74.0 0.0 collective-permute-done.7.refs_4_
  74.0 4.2 %collective-permute-start.17 = (bf16[2,2,64,512]{3,2,1,0:T(8,128)(2,1)S(1)}, bf16[2,2,64,512]{3,2,1,0:T(8,128)(2,1)S(1)}, u32[]{:S(2)}, u32[]{:S(2)}) collective-permute-start(bf16[2,2,64,512]{3,2,1,0:T(8,128)(2,1)S(1)} %get-tuple-element.43), channel_id=1, source_target_pairs={{0,80},{8,88},{16,96},{24,104},{32,112},{40,120},{48,0},{56,8},{64... | collective-permute-start | bytes 786440 | tf_op jit(solution)/shard_map/ppermute | solution.py:24
  78.3 0.0 collective-permute-done.8.refs_5_
  78.3 4.5 %collective-permute-start.9 = (bf16[2,2,64,512]{3,2,1,0:T(8,128)(2,1)S(1)}, bf16[2,2,64,512]{3,2,1,0:T(8,128)(2,1)S(1)}, u32[]{:S(2)}, u32[]{:S(2)}) collective-permute-start(bf16[2,2,64,512]{3,2,1,0:T(8,128)(2,1)S(1)} %get-tuple-element.34), channel_id=1, source_target_pairs={{0,128},{8,136},{16,144},{24,152},{32,160},{40,168},{48,176},{56,1... | collective-permute-start | bytes 786440 | tf_op jit(solution)/shard_map/ppermute | solution.py:24
  82.8 11.7 %collective-permute-done.14.refs_7_ = bf16[2,2,64,512]{3,2,1,0:T(8,128)(2,1)S(1)} collective-permute-done((bf16[2,2,64,512]{3,2,1,0:T(8,128)(2,1)S(1)}, bf16[2,2,64,512]{3,2,1,0:T(8,128)(2,1)S(1)}, u32[]{:S(2)}, u32[]{:S(2)}) %collective-permute-start.14) | collective-permute-done | bytes 262176 | tf_op jit(solution)/shard_map/ppermute | solution.py:24
  94.4 5.0 %collective-permute-start.1 = (bf16[2,2,64,512]{3,2,1,0:T(8,128)(2,1)S(1)}, bf16[2,2,64,512]{3,2,1,0:T(8,128)(2,1)S(1)}, u32[]{:S(2)}, u32[]{:S(2)}) collective-permute-start(bf16[2,2,64,512]{3,2,1,0:T(8,128)(2,1)S(1)} %get-tuple-element.26), channel_id=1, source_target_pairs={{0,144},{8,152},{16,160},{24,168},{32,176},{40,184},{48,192},{56,2... | collective-permute-start | bytes 786440 | tf_op jit(solution)/shard_map/ppermute | solution.py:24
  99.5 1.5 %collective-permute-done.15.refs_8_ = bf16[2,2,64,512]{3,2,1,0:T(8,128)(2,1)S(1)} collective-permute-done((bf16[2,2,64,512]{3,2,1,0:T(8,128)(2,1)S(1)}, bf16[2,2,64,512]{3,2,1,0:T(8,128)(2,1)S(1)}, u32[]{:S(2)}, u32[]{:S(2)}) %collective-permute-start.15) | collective-permute-done | bytes 262176 | tf_op jit(solution)/shard_map/ppermute | solution.py:24
  101.0 0.0 collective-permute-start.2
  101.0 0.0 collective-permute-done.16.refs_9_
  101.0 3.4 %collective-permute-start.3 = (bf16[2,2,64,512]{3,2,1,0:T(8,128)(2,1)S(1)}, bf16[2,2,64,512]{3,2,1,0:T(8,128)(2,1)S(1)}, u32[]{:S(2)}, u32[]{:S(2)}) collective-permute-start(bf16[2,2,64,512]{3,2,1,0:T(8,128)(2,1)S(1)} %get-tuple-element.28), channel_id=1, source_target_pairs={{0,16},{8,24},{16,32},{24,40},{32,48},{40,56},{48,64},{56,72},{64,... | collective-permute-start | bytes 786440 | tf_op jit(solution)/shard_map/ppermute | solution.py:24
  104.5 2.5 %collective-permute-done.17.refs_10_ = bf16[2,2,64,512]{3,2,1,0:T(8,128)(2,1)S(1)} collective-permute-done((bf16[2,2,64,512]{3,2,1,0:T(8,128)(2,1)S(1)}, bf16[2,2,64,512]{3,2,1,0:T(8,128)(2,1)S(1)}, u32[]{:S(2)}, u32[]{:S(2)}) %collective-permute-start.17) | collective-permute-done | bytes 262176 | tf_op jit(solution)/shard_map/ppermute | solution.py:24
  106.9 3.0 %collective-permute-start.4 = (bf16[2,2,64,512]{3,2,1,0:T(8,128)(2,1)S(1)}, bf16[2,2,64,512]{3,2,1,0:T(8,128)(2,1)S(1)}, u32[]{:S(2)}, u32[]{:S(2)}) collective-permute-start(bf16[2,2,64,512]{3,2,1,0:T(8,128)(2,1)S(1)} %get-tuple-element.29), channel_id=1, source_target_pairs={{0,112},{8,120},{16,0},{24,8},{32,16},{40,24},{48,32},{56,40},{64,... | collective-permute-start | bytes 786440 | tf_op jit(solution)/shard_map/ppermute | solution.py:24
  110.0 0.0 copy-done.2
  110.0 0.0 copy-done.1
  110.0 3.2 %shard_map.53 = (bf16[2,2048,512]{2,1,0:T(8,128)(2,1)}, f32[2,8,512]{2,1,0:T(8,128)S(1)}) custom-call(s32[16]{0:T(128)S(1)} %bitcast.1, s32[8,2048]{1,0:T(8,128)S(1)} %copy-done.1, bf16[2,2,64,512]{3,2,1,0:T(8,128)(2,1)S(1)} %get-tuple-element.35.refs_2_, bf16[2,64,512]{2,1,0:T(8,128)(2,1)S(1)} %collective-permute-done.10.refs_3_, ...), custom_call_target="tpu_custom_call" | custom-call | flops 14680064 | bytes 3670016 | tf_op jit(solution)/shard_map/pallas_call | solution.py:190
  113.2 0.0 collective-permute-done.9.refs_6_
  113.2 2.7 %shard_map.54 = (bf16[2,2048,512]{2,1,0:T(8,128)(2,1)}, f32[2,8,512]{2,1,0:T(8,128)S(1)}) custom-call(s32[16]{0:T(128)S(1)} %bitcast.2, s32[8,2048]{1,0:T(8,128)S(1)} %copy-done.1, bf16[2,2,64,512]{3,2,1,0:T(8,128)(2,1)S(1)} %collective-permute-done.5.refs_2_, ...), custom_call_target="tpu_custom_call", output_to_operand_aliasing={{0}: (8, {})} | custom-call | flops 10485760 | bytes 2621440 | tf_op jit(solution)/shard_map/pallas_call | solution.py:190
  115.9 0.0 collective-permute-done.1.refs_2_
  115.9 0.6 collective-permute-done.2.refs_3_
  116.5 4.7 %collective-permute-done.3.refs_4_ = bf16[2,2,64,512]{3,2,1,0:T(8,128)(2,1)S(1)} collective-permute-done((bf16[2,2,64,512]{3,2,1,0:T(8,128)(2,1)S(1)}, bf16[2,2,64,512]{3,2,1,0:T(8,128)(2,1)S(1)}, u32[]{:S(2)}, u32[]{:S(2)}) %collective-permute-start.3) | collective-permute-done | bytes 262176 | tf_op jit(solution)/shard_map/ppermute | solution.py:24
  121.2 2.1 %collective-permute-done.4.refs_5_ = bf16[2,2,64,512]{3,2,1,0:T(8,128)(2,1)S(1)} collective-permute-done((bf16[2,2,64,512]{3,2,1,0:T(8,128)(2,1)S(1)}, bf16[2,2,64,512]{3,2,1,0:T(8,128)(2,1)S(1)}, u32[]{:S(2)}, u32[]{:S(2)}) %collective-permute-start.4) | collective-permute-done | bytes 262176 | tf_op jit(solution)/shard_map/ppermute | solution.py:24
  123.3 2.4 %shard_map.55 = (bf16[2,2048,512]{2,1,0:T(8,128)(2,1)}, f32[8,8,128]{2,1,0:T(8,128)S(1)}) custom-call(s32[16]{0:T(128)S(1)} %bitcast.3, s32[8,2048]{1,0:T(8,128)S(1)} %copy-done.1, bf16[2,2,64,512]{3,2,1,0:T(8,128)(2,1)S(1)} %collective-permute-done.1.refs_2_, ...), custom_call_target="tpu_custom_call", output_to_operand_aliasing={{0}: (7, {})} | custom-call | flops 8388608 | bytes 2097152 | tf_op jit(solution)/shard_map/pallas_call | solution.py:190
  125.7 11.5 %all_to_all.5.parts_ref = f32[8,8,128]{2,1,0:T(8,128)} all-to-all(f32[8,8,128]{2,1,0:T(8,128)S(1)} %get-tuple-element.49), channel_id=1, replica_groups=mesh['dp'=32,'tensor'=8] {'tensor'}, dimensions={0} | all-to-all | bytes 65536 | tf_op jit(solution)/shard_map/all_to_all | solution.py:249
  137.2 1.4 %total.1 = f32[2,8,64]{2,1,0:T(8,128)} custom-call(f32[8,8,128]{2,1,0:T(8,128)} %all_to_all.5.parts_ref), custom_call_target="tpu_custom_call" | custom-call | tf_op jit(solution)/shard_map/total/pallas_call | solution.py:251
Async XLA Ops:
  3.8 9.5 %collective-permute-start = (bf16[14,2,64,512]{3,2,1,0:T(8,128)(2,1)}, bf16[14,2,64,512]{3,2,1,0:T(8,128)(2,1)S(1)}, u32[]{:S(2)}, u32[]{:S(2)}) collective-permute-start(bf16[14,2,64,512]{3,2,1,0:T(8,128)(2,1)} %shard_map.50), channel_id=1, source_target_pairs={{0,8},{8,0},{16,24},{24,16},{32,40},{40,32},{48,56},{56,48},{64,72... | collective-permute-start | bytes 5505032 | tf_op jit(solution)/shard_map/ppermute | solution.py:24
  5.8 26.6 %collective-permute-start.10 = (bf16[2,64,512]{2,1,0:T(8,128)(2,1)}, bf16[2,64,512]{2,1,0:T(8,128)(2,1)S(1)}, u32[]{:S(2)}, u32[]{:S(2)}) collective-permute-start(bf16[2,64,512]{2,1,0:T(8,128)(2,1)} %get-tuple-element.36), channel_id=1, source_target_pairs={{0,64},{8,72},{16,80},{24,88},{32,96},{40,104},{48,112},{56,120},{... | collective-permute-start | bytes 393224 | tf_op jit(solution)/shard_map/ppermute | solution.py:24
  13.1 96.9 %copy-start.2 = (s32[1,16]{1,0:T(1,128)S(1)}, s32[1,16]{1,0:T(1,128)}, u32[]{:S(2)}) copy-start(s32[1,16]{1,0:T(1,128)} %param.4) | copy-start | bytes 196
  13.1 24.7 %collective-permute-start.11 = (bf16[2,64,512]{2,1,0:T(8,128)(2,1)}, bf16[2,64,512]{2,1,0:T(8,128)(2,1)S(1)}, u32[]{:S(2)}, u32[]{:S(2)}) collective-permute-start(bf16[2,64,512]{2,1,0:T(8,128)(2,1)} %get-tuple-element.37), channel_id=1, source_target_pairs={{0,72},{8,64},{16,88},{24,80},{32,104},{40,96},{48,120},{56,112},{... | collective-permute-start | bytes 393224 | tf_op jit(solution)/shard_map/ppermute | solution.py:24
  13.3 3.4 %copy-start = (f32[2,64,16384]{2,1,0:T(8,128)S(1)}, f32[2,64,16384]{2,1,0:T(8,128)}, u32[]{:S(2)}) copy-start(f32[2,64,16384]{2,1,0:T(8,128)} %refs_0_.5) | copy-start | bytes 25165828
  16.7 15.8 %copy-start.4 = (bf16[2,64,512]{2,1,0:T(8,128)(2,1)S(1)}, bf16[2,64,512]{2,1,0:T(8,128)(2,1)}, u32[]{:S(2)}) copy-start(bf16[2,64,512]{2,1,0:T(8,128)(2,1)} %get-tuple-element.38) | copy-start | bytes 393220
  16.7 21.1 %copy-start.3 = (bf16[2,64,512]{2,1,0:T(8,128)(2,1)S(1)}, bf16[2,64,512]{2,1,0:T(8,128)(2,1)}, u32[]{:S(2)}) copy-start(bf16[2,64,512]{2,1,0:T(8,128)(2,1)} %get-tuple-element.39) | copy-start | bytes 393220
  16.7 93.3 %copy-start.1 = (s32[8,2048]{1,0:T(8,128)S(1)}, s32[8,2048]{1,0:T(8,128)}, u32[]{:S(2)}) copy-start(s32[8,2048]{1,0:T(8,128)} %refs_1_.5) | copy-start | bytes 196612
  25.4 40.4 %collective-permute-start.5 = (bf16[2,2,64,512]{3,2,1,0:T(8,128)(2,1)S(1)}, bf16[2,2,64,512]{3,2,1,0:T(8,128)(2,1)S(1)}, u32[]{:S(2)}, u32[]{:S(2)}) collective-permute-start(bf16[2,2,64,512]{3,2,1,0:T(8,128)(2,1)S(1)} %get-tuple-element.30), channel_id=1, source_target_pairs={{0,160},{8,168},{16,176},{24,184},{32,192},{40,200},{48,208},{56,2... | collective-permute-start | bytes 786440 | tf_op jit(solution)/shard_map/ppermute | solution.py:24
  27.0 46.2 %collective-permute-start.6 = (bf16[2,2,64,512]{3,2,1,0:T(8,128)(2,1)S(1)}, bf16[2,2,64,512]{3,2,1,0:T(8,128)(2,1)S(1)}, u32[]{:S(2)}, u32[]{:S(2)}) collective-permute-start(bf16[2,2,64,512]{3,2,1,0:T(8,128)(2,1)S(1)} %get-tuple-element.31), channel_id=1, source_target_pairs={{0,224},{8,232},{16,240},{24,248},{32,128},{40,136},{48,144},{56,1... | collective-permute-start | bytes 786440 | tf_op jit(solution)/shard_map/ppermute | solution.py:24
  32.0 42.0 %collective-permute-start.7 = (bf16[2,2,64,512]{3,2,1,0:T(8,128)(2,1)S(1)}, bf16[2,2,64,512]{3,2,1,0:T(8,128)(2,1)S(1)}, u32[]{:S(2)}, u32[]{:S(2)}) collective-permute-start(bf16[2,2,64,512]{3,2,1,0:T(8,128)(2,1)S(1)} %get-tuple-element.32), channel_id=1, source_target_pairs={{0,32},{8,40},{16,48},{24,56},{32,64},{40,72},{48,80},{56,88},{64,... | collective-permute-start | bytes 786440 | tf_op jit(solution)/shard_map/ppermute | solution.py:24
  32.4 23.4 %collective-permute-start.12 = (bf16[2,64,512]{2,1,0:T(8,128)(2,1)S(1)}, bf16[2,64,512]{2,1,0:T(8,128)(2,1)S(1)}, u32[]{:S(2)}, u32[]{:S(2)}) collective-permute-start(bf16[2,64,512]{2,1,0:T(8,128)(2,1)S(1)} %copy-done.4), channel_id=1, source_target_pairs={{0,192},{8,200},{16,208},{24,216},{32,224},{40,232},{48,240},{56,2... | collective-permute-start | bytes 393224 | tf_op jit(solution)/shard_map/ppermute | solution.py:24
  37.8 28.0 %collective-permute-start.13 = (bf16[2,64,512]{2,1,0:T(8,128)(2,1)S(1)}, bf16[2,64,512]{2,1,0:T(8,128)(2,1)S(1)}, u32[]{:S(2)}, u32[]{:S(2)}) collective-permute-start(bf16[2,64,512]{2,1,0:T(8,128)(2,1)S(1)} %copy-done.3), channel_id=1, source_target_pairs={{0,200},{8,192},{16,216},{24,208},{32,232},{40,224},{48,248},{56,2... | collective-permute-start | bytes 393224 | tf_op jit(solution)/shard_map/ppermute | solution.py:24
  55.8 22.5 %collective-permute-start.8 = (bf16[2,2,64,512]{3,2,1,0:T(8,128)(2,1)S(1)}, bf16[2,2,64,512]{3,2,1,0:T(8,128)(2,1)S(1)}, u32[]{:S(2)}, u32[]{:S(2)}) collective-permute-start(bf16[2,2,64,512]{3,2,1,0:T(8,128)(2,1)S(1)} %get-tuple-element.33), channel_id=1, source_target_pairs={{0,96},{8,104},{16,112},{24,120},{32,0},{40,8},{48,16},{56,24},{64... | collective-permute-start | bytes 786440 | tf_op jit(solution)/shard_map/ppermute | solution.py:24
  65.8 28.6 %collective-permute-start.14 = (bf16[2,2,64,512]{3,2,1,0:T(8,128)(2,1)S(1)}, bf16[2,2,64,512]{3,2,1,0:T(8,128)(2,1)S(1)}, u32[]{:S(2)}, u32[]{:S(2)}) collective-permute-start(bf16[2,2,64,512]{3,2,1,0:T(8,128)(2,1)S(1)} %get-tuple-element.40), channel_id=1, source_target_pairs={{0,176},{8,184},{16,192},{24,200},{32,208},{40,216},{48,224},{56,2... | collective-permute-start | bytes 786440 | tf_op jit(solution)/shard_map/ppermute | solution.py:24
  65.8 35.2 %collective-permute-start.15 = (bf16[2,2,64,512]{3,2,1,0:T(8,128)(2,1)S(1)}, bf16[2,2,64,512]{3,2,1,0:T(8,128)(2,1)S(1)}, u32[]{:S(2)}, u32[]{:S(2)}) collective-permute-start(bf16[2,2,64,512]{3,2,1,0:T(8,128)(2,1)S(1)} %get-tuple-element.41), channel_id=1, source_target_pairs={{0,208},{8,216},{16,224},{24,232},{32,240},{40,248},{48,128},{56,1... | collective-permute-start | bytes 786440 | tf_op jit(solution)/shard_map/ppermute | solution.py:24
  73.2 27.8 %collective-permute-start.16 = (bf16[2,2,64,512]{3,2,1,0:T(8,128)(2,1)S(1)}, bf16[2,2,64,512]{3,2,1,0:T(8,128)(2,1)S(1)}, u32[]{:S(2)}, u32[]{:S(2)}) collective-permute-start(bf16[2,2,64,512]{3,2,1,0:T(8,128)(2,1)S(1)} %get-tuple-element.42), channel_id=1, source_target_pairs={{0,48},{8,56},{16,64},{24,72},{32,80},{40,88},{48,96},{56,104},{64... | collective-permute-start | bytes 786440 | tf_op jit(solution)/shard_map/ppermute | solution.py:24
  74.0 32.9 %collective-permute-start.17 = (bf16[2,2,64,512]{3,2,1,0:T(8,128)(2,1)S(1)}, bf16[2,2,64,512]{3,2,1,0:T(8,128)(2,1)S(1)}, u32[]{:S(2)}, u32[]{:S(2)}) collective-permute-start(bf16[2,2,64,512]{3,2,1,0:T(8,128)(2,1)S(1)} %get-tuple-element.43), channel_id=1, source_target_pairs={{0,80},{8,88},{16,96},{24,104},{32,112},{40,120},{48,0},{56,8},{64... | collective-permute-start | bytes 786440 | tf_op jit(solution)/shard_map/ppermute | solution.py:24
  78.3 34.9 %collective-permute-start.9 = (bf16[2,2,64,512]{3,2,1,0:T(8,128)(2,1)S(1)}, bf16[2,2,64,512]{3,2,1,0:T(8,128)(2,1)S(1)}, u32[]{:S(2)}, u32[]{:S(2)}) collective-permute-start(bf16[2,2,64,512]{3,2,1,0:T(8,128)(2,1)S(1)} %get-tuple-element.34), channel_id=1, source_target_pairs={{0,128},{8,136},{16,144},{24,152},{32,160},{40,168},{48,176},{56,1... | collective-permute-start | bytes 786440 | tf_op jit(solution)/shard_map/ppermute | solution.py:24
  94.4 21.5 %collective-permute-start.1 = (bf16[2,2,64,512]{3,2,1,0:T(8,128)(2,1)S(1)}, bf16[2,2,64,512]{3,2,1,0:T(8,128)(2,1)S(1)}, u32[]{:S(2)}, u32[]{:S(2)}) collective-permute-start(bf16[2,2,64,512]{3,2,1,0:T(8,128)(2,1)S(1)} %get-tuple-element.26), channel_id=1, source_target_pairs={{0,144},{8,152},{16,160},{24,168},{32,176},{40,184},{48,192},{56,2... | collective-permute-start | bytes 786440 | tf_op jit(solution)/shard_map/ppermute | solution.py:24
  101.0 15.5 %collective-permute-start.2 = (bf16[2,2,64,512]{3,2,1,0:T(8,128)(2,1)S(1)}, bf16[2,2,64,512]{3,2,1,0:T(8,128)(2,1)S(1)}, u32[]{:S(2)}, u32[]{:S(2)}) collective-permute-start(bf16[2,2,64,512]{3,2,1,0:T(8,128)(2,1)S(1)} %get-tuple-element.27), channel_id=1, source_target_pairs={{0,240},{8,248},{16,128},{24,136},{32,144},{40,152},{48,160},{56,1... | collective-permute-start | bytes 786440 | tf_op jit(solution)/shard_map/ppermute | solution.py:24
  101.0 20.2 %collective-permute-start.3 = (bf16[2,2,64,512]{3,2,1,0:T(8,128)(2,1)S(1)}, bf16[2,2,64,512]{3,2,1,0:T(8,128)(2,1)S(1)}, u32[]{:S(2)}, u32[]{:S(2)}) collective-permute-start(bf16[2,2,64,512]{3,2,1,0:T(8,128)(2,1)S(1)} %get-tuple-element.28), channel_id=1, source_target_pairs={{0,16},{8,24},{16,32},{24,40},{32,48},{40,56},{48,64},{56,72},{64,... | collective-permute-start | bytes 786440 | tf_op jit(solution)/shard_map/ppermute | solution.py:24
  106.9 16.4 %collective-permute-start.4 = (bf16[2,2,64,512]{3,2,1,0:T(8,128)(2,1)S(1)}, bf16[2,2,64,512]{3,2,1,0:T(8,128)(2,1)S(1)}, u32[]{:S(2)}, u32[]{:S(2)}) collective-permute-start(bf16[2,2,64,512]{3,2,1,0:T(8,128)(2,1)S(1)} %get-tuple-element.29), channel_id=1, source_target_pairs={{0,112},{8,120},{16,0},{24,8},{32,16},{40,24},{48,32},{56,40},{64,... | collective-permute-start | bytes 786440 | tf_op jit(solution)/shard_map/ppermute | solution.py:24

commit v3 on v0

v3 whole, which is shorter than its diff:
```python
import functools

import jax
import jax.numpy as jnp
from jax import lax
from jax.experimental import pallas as pl
from jax.experimental.pallas import tpu as pltpu
from jax.sharding import PartitionSpec as P


NX, NZ = 2, 8
DIRECT = ((0, 4), (1, 4))
FIRST = ((1, 3), (1, 5), (0, 3), (0, 5))
SECOND = ((1, 2), (1, 6), (0, 2), (0, 6))
THIRD = ((1, 0), (1, 1), (1, 7), (0, 1), (0, 7))
EXTRA = 8
GRANT = 12 * 2**20
PACK_GRANT = 50 * 2**20

VMEM = pl.BlockSpec(memory_space=pltpu.VMEM)
SMEM = pl.BlockSpec(memory_space=pltpu.SMEM)
HBM = pl.BlockSpec(memory_space=pltpu.HBM)
ANY = pl.BlockSpec(memory_space=pl.ANY)


def send(array, delta):
    return lax.ppermute(array, "dp", shift(*delta))


def exchange(array):
    return lax.all_to_all(array, "tensor", split_axis=0, concat_axis=0, tiled=True)


def position():
    me = lax.axis_index("dp")
    core = lax.rem(me, 2)
    chip = me // 2
    return chip // NZ, lax.rem(chip, NZ), core


def device_at(dx, dz, dc):
    x, z, core = position()
    return (lax.rem(x + dx, NX) * NZ + lax.rem(z + dz, NZ)) * 2 + lax.rem(core + dc, 2)


def sender(dx, dz):
    x, z, _ = position()
    return lax.rem(x + NX - dx, NX) * NZ + lax.rem(z + NZ - dz, NZ)


def shift(dx, dz, dc):
    pairs = []
    for x in range(NX):
        for z in range(NZ):
            for core in range(2):
                target = ((x + dx) % NX * NZ + (z + dz) % NZ) * 2 + (core + dc) % 2
                pairs.append(((x * NZ + z) * 2 + core, target))
    return pairs


def place_of(order_ref, place):
    for k in range(order_ref.shape[0]):
        place[order_ref[k]] = k


def tile_weights(weights_ref, k, tile_rows):
    start = pl.multiple_of(k * tile_rows, tile_rows)
    weights = weights_ref[:, pl.ds(start, tile_rows)].astype(jnp.float32)
    half = tile_rows // 2
    turned = jnp.concatenate([weights[:, half:], weights[:, :half]], axis=1)
    core = position()[2]
    return jnp.where(core == 0, weights, turned).astype(jnp.bfloat16)


def by_owner(sums, groups):
    each = sums[0].shape[1] // groups
    return [jnp.concatenate([s[:, t * each:(t + 1) * each] for s in sums], axis=1) for t in range(groups)]


def pack_kernel(blocks, copies, n_out, summed, *refs):
    refs = list(refs)
    master_ref = refs.pop(0)
    swapped_ref = refs.pop(0) if copies else None
    if summed:
        order_ref, weights_ref = refs.pop(0), refs.pop(0)
    outs, refs = refs[:n_out], refs[n_out:]
    if summed:
        sums_ref = refs.pop(0)
        place = refs.pop()
    wide, sems = refs
    layers, rows, columns = wide.shape[1:]

    def fetch(i):
        start = pl.multiple_of(device_at(*blocks[i][0]) * columns, columns)
        return pltpu.make_async_copy(master_ref.at[:, :, pl.ds(start, columns)], wide.at[i], sems.at[i])

    for i in range(len(blocks)):
        fetch(i).start()
    for source, out, offset, stride in copies:
        for l in range(layers):
            outs[out][offset + l * stride:offset + l * stride + rows] = swapped_ref[source, l]
    if summed:
        place_of(order_ref, place)
        x, z, _ = position()
        weights = tile_weights(weights_ref, place[x * NZ + z], 2 * rows)
    done = 0
    for i, (_, out, offset, stride) in enumerate(blocks):
        fetch(i).wait()
        for l in range(layers):
            low = wide[i, l].astype(jnp.bfloat16)
            if isinstance(offset, tuple):
                outs[out][offset[0], l] = low
            else:
                outs[out][offset + l * stride:offset + l * stride + rows] = low
        if out in summed:
            tile = [outs[out][l * 2 * rows:(l + 1) * 2 * rows] for l in range(layers)]
            sums = [jnp.dot(weights, t, preferred_element_type=jnp.float32) for t in tile]
            for t, part in enumerate(by_owner(sums, sums_ref.shape[0])):
                sums_ref[t, done] = part
            done += 1


def pack(master, parts, blocks, shapes, swapped=None, copies=(), summed=(), checks=None, grant=PACK_GRANT):
    layers, rows, width = master.shape
    columns = width // parts
    operands, specs = [master], [HBM]
    if copies:
        operands.append(swapped)
        specs.append(VMEM)
    out_shape = [jax.ShapeDtypeStruct(s, jnp.bfloat16) for s in shapes]
    scratch = [
        pltpu.VMEM((len(blocks), layers, rows, columns), jnp.float32),
        pltpu.SemaphoreType.DMA((len(blocks),)),
    ]
    flops = 0
    if summed:
        order, weights, groups = checks
        operands += [order, weights]
        specs += [SMEM, VMEM]
        out_shape.append(
            jax.ShapeDtypeStruct((groups, len(summed), weights.shape[0], layers * columns // groups), jnp.float32)
        )
        scratch.append(pltpu.SMEM((order.shape[0],), jnp.int32))
        flops = 2 * len(summed) * weights.shape[0] * layers * 2 * rows * columns
    piece = layers * rows * columns * 2
    return pl.pallas_call(
        functools.partial(pack_kernel, blocks, copies, len(shapes), summed),
        in_specs=specs,
        out_specs=[VMEM] * len(out_shape),
        out_shape=out_shape,
        scratch_shapes=scratch,
        cost_estimate=pl.CostEstimate(
            flops=flops, transcendentals=0, bytes_accessed=piece * (3 * len(blocks) + 2 * len(copies))
        ),
        compiler_params=pltpu.CompilerParams(vmem_limit_bytes=grant),
    )(*operands)


def put_tile(piece, tiled_ref, k, layers, rows, sems, split):
    core = position()[2]
    copies = []
    for slot in range(2):
        half = core if slot == 0 else 1 - core
        start = pl.multiple_of(k * 2 * rows + half * rows, rows)
        for l in range(layers):
            at = l * rows if split else (2 * l + slot) * rows
            source = piece[slot if split else 0].at[pl.ds(at, rows)]
            target = tiled_ref.at[l, pl.ds(start, rows)]
            copies.append(pltpu.make_async_copy(source, target, sems.at[slot, l]))
    return copies


def regroup_kernel(chips, aliased, groups, rows, *refs):
    refs = list(refs)
    order_ref, weights_ref = refs.pop(0), refs.pop(0)
    pieces = []
    for _, split in chips:
        pieces.append([refs.pop(0) for _ in range(2 if split else 1)])
    if aliased:
        sums_in = refs.pop(0)
        refs.pop(0)
    tiled_ref, sums_ref, place, sems = refs
    layers, _, columns = tiled_ref.shape
    place_of(order_ref, place)
    where = [place[sender(*delta)] for delta, _ in chips]
    copies = []
    for i, (_, split) in enumerate(chips):
        copies += put_tile(pieces[i], tiled_ref, where[i], layers, rows, sems.at[i], split)
    for copy in copies:
        copy.start()
    checks = weights_ref.shape[0]
    sums = [sums_in[l] if aliased else jnp.zeros((checks, columns), jnp.float32) for l in range(layers)]
    for i, (_, split) in enumerate(chips):
        weights = tile_weights(weights_ref, where[i], 2 * rows)
        for l in range(layers):
            if split:
                for slot in range(2):
                    sums[l] += jnp.dot(
                        weights[:, slot * rows:(slot + 1) * rows],
                        pieces[i][slot][l * rows:(l + 1) * rows],
                        preferred_element_type=jnp.float32,
                    )
            else:
                sums[l] += jnp.dot(
                    weights, pieces[i][0][2 * l * rows:2 * (l + 1) * rows], preferred_element_type=jnp.float32
                )
    if groups:
        for t, part in enumerate(by_owner(sums, groups)):
            sums_ref[t] = part
    else:
        for l in range(layers):
            sums_ref[l] = sums[l]
    for copy in copies:
        copy.wait()


def regroup(order, weights, pieces, chips, shape, before, groups):
    layers, height, columns = shape
    count = order.shape[0]
    checks = weights.shape[0]
    rows = height // count // 2
    operands = [order, weights, *pieces]
    specs = [SMEM, VMEM] + [VMEM] * len(pieces)
    aliases = {}
    if before is not None:
        tiled, sums = before
        operands += [sums, tiled]
        specs += [VMEM, HBM]
        aliases = {len(operands) - 1: 0}
    sums_shape = (groups, checks, layers * columns // groups) if groups else (layers, checks, columns)
    n = len(chips)
    return pl.pallas_call(
        functools.partial(regroup_kernel, chips, before is not None, groups, rows),
        in_specs=specs,
        out_specs=[HBM, VMEM],
        out_shape=[jax.ShapeDtypeStruct(shape, jnp.bfloat16), jax.ShapeDtypeStruct(sums_shape, jnp.float32)],
        scratch_shapes=[pltpu.SMEM((count,), jnp.int32), pltpu.SemaphoreType.DMA((n, 2, layers))],
        input_output_aliases=aliases,
        cost_estimate=pl.CostEstimate(
            flops=2 * n * checks * layers * 2 * rows * columns,
            transcendentals=0,
            bytes_accessed=2 * n * layers * 2 * rows * columns * 2,
        ),
        compiler_params=pltpu.CompilerParams(vmem_limit_bytes=GRANT),
    )(*operands)


def attach_kernel(parts_ref, *refs):
    n = parts_ref.shape[1]
    outs = refs[n:2 * n]
    extra, sems = refs[2 * n:]
    copies = []
    for i in range(n):
        total = parts_ref[0, i]
        for g in range(1, parts_ref.shape[0]):
            total += parts_ref[g, i]
        high = total.astype(jnp.bfloat16)
        rest = total - high.astype(jnp.float32)
        middle = rest.astype(jnp.bfloat16)
        low = (rest - middle.astype(jnp.float32)).astype(jnp.bfloat16)
        extra[i] = jnp.concatenate([high, middle, low, jnp.zeros_like(low)], axis=1)
        height = outs[i].shape[0]
        copies.append(pltpu.make_async_copy(extra.at[i], outs[i].at[pl.ds(height - EXTRA, EXTRA)], sems.at[i]))
        copies[-1].start()
    for copy in copies:
        copy.wait()


def attach(parts, pieces):
    n = len(pieces)
    return pl.pallas_call(
        attach_kernel,
        in_specs=[VMEM] + [ANY] * n,
        out_specs=[ANY] * n,
        out_shape=[jax.ShapeDtypeStruct(p.shape, p.dtype) for p in pieces],
        scratch_shapes=[pltpu.VMEM((n, EXTRA, pieces[0].shape[1]), jnp.bfloat16), pltpu.SemaphoreType.DMA((n,))],
        input_output_aliases={i + 1: i for i in range(n)},
        compiler_params=pltpu.CompilerParams(vmem_limit_bytes=GRANT),
        cost_estimate=pl.CostEstimate(flops=0, transcendentals=0, bytes_accessed=parts.size * 4),
        name="attach",
    )(parts, *pieces)


def finish_kernel(chips, rows, *refs):
    refs = list(refs)
    order_ref, parts_ref = refs.pop(0), refs.pop(0)
    pieces, refs = refs[:len(chips)], refs[len(chips) + 1:]
    tiled_ref, checksum_ref, place, sems = refs
    layers = tiled_ref.shape[0]
    place_of(order_ref, place)
    copies = []
    for i, delta in enumerate(chips):
        copies += put_tile([pieces[i]], tiled_ref, place[sender(*delta)], layers, rows, sems.at[i], False)
    for copy in copies:
        copy.start()
    total = parts_ref[0]
    for g in range(1, parts_ref.shape[0]):
        total += parts_ref[g]
    width = total.shape[1]
    for piece in pieces:
        extra = piece[piece.shape[0] - EXTRA:].astype(jnp.float32)
        total += extra[:, :width] + (extra[:, width:2 * width] + extra[:, 2 * width:3 * width])
    each = width // layers
    for l in range(layers):
        checksum_ref[l] = total[:, l * each:(l + 1) * each]
    for copy in copies:
        copy.wait()


def finish(order, parts, pieces, chips, tiled):
    layers, height, _ = tiled.shape
    count = order.shape[0]
    rows = height // count // 2
    _, checks, width = parts.shape
    n = len(chips)
    return pl.pallas_call(
        functools.partial(finish_kernel, chips, rows),
        in_specs=[SMEM, VMEM] + [VMEM] * n + [HBM],
        out_specs=[HBM, VMEM],
        out_shape=[
            jax.ShapeDtypeStruct(tiled.shape, tiled.dtype),
            jax.ShapeDtypeStruct((layers, checks, width // layers), jnp.float32),
        ],
        scratch_shapes=[pltpu.SMEM((count,), jnp.int32), pltpu.SemaphoreType.DMA((n, 2, layers))],
        input_output_aliases={2 + n: 0},
        compiler_params=pltpu.CompilerParams(vmem_limit_bytes=GRANT),
        name="finish",
    )(order, parts, *pieces, tiled)


def on_device(parts, groups, master, tile_order, check_weights):
    layers, rows, width = master.shape
    columns = width // parts
    order = tile_order[0]
    shape = (layers, check_weights.shape[1], columns)
    whole = (layers * 2 * rows, columns)
    longer = (layers * 2 * rows + EXTRA, columns)

    blocks = tuple((d + (dc,), 2 * i + dc, 0, rows) for i, d in enumerate(DIRECT) for dc in range(2))
    direct = pack(master, parts, blocks, [(layers * rows, columns)] * len(blocks))
    direct = [send(a, b[0]) for a, b in zip(direct, blocks)]

    mine = FIRST + ((0, 0),) + SECOND + THIRD
    blocks = tuple((d + (1,), 0, (i,), 0) for i, d in enumerate(mine))
    (sibling,) = pack(master, parts, blocks, [(len(mine), layers, rows, columns)])
    swapped = send(sibling, (0, 0, 1))

    n = len(FIRST)
    blocks = tuple((d + (0,), i, 0, 2 * rows) for i, d in enumerate(FIRST))
    copies = tuple((i, i, rows, 2 * rows) for i in range(n))
    first = pack(master, parts, blocks, [whole] * n, swapped, copies)
    first = [send(a, d + (0,)) for d, a in zip(FIRST, first)]

    rest = mine[n:]
    blocks = tuple((d + (0,), i, 0, 2 * rows) for i, d in enumerate(rest))
    copies = tuple((n + i, i, rows, 2 * rows) for i in range(len(rest)))
    shapes = [whole] * (1 + len(SECOND)) + [longer] * len(THIRD)
    summed = tuple(range(1 + len(SECOND), len(rest)))
    here, *rest, sums = pack(master, parts, blocks, shapes, swapped, copies, summed, (order, check_weights, groups))
    second = [send(a, d + (0,)) for d, a in zip(SECOND, rest)]
    late = attach(exchange(sums), rest[len(SECOND):])
    third = [send(a, d + (0,)) for d, a in zip(THIRD, late)]

    chips = (((0, 0), False),) + tuple((d, True) for d in DIRECT) + tuple((d, False) for d in FIRST)
    state = regroup(order, check_weights, [here, *direct, *first], chips, shape, None, 0)
    chips = tuple((d, False) for d in SECOND)
    tiled, sums = regroup(order, check_weights, second, chips, shape, state, groups)
    return tuple(finish(order, exchange(sums), third, THIRD, tiled))


def solution(mesh):
    in_specs = (P(None, ("tensor", "dp"), None), P("tensor", None), P(None, "tensor"))
    out_specs = (P(None, "tensor", "dp"), P(None, None, ("dp", "tensor")))

    def body(*args):
        return on_device(mesh.shape["dp"], mesh.shape["tensor"], *args)

    return jax.shard_map(body, mesh=mesh, in_specs=in_specs, out_specs=out_specs, check_vma=False)
```

time: 246 us -> 128 us (0.52)
  waiting for transfers between devices: 135 us -> 36.8 us
  local copies, waits for them, and re-layouts: 76.3 us -> 0.01 us
  starting transfers between devices: 11.8 us -> 43.8 us
  blocking collectives: 0 us -> 29 us
  Pallas kernels: 0 us -> 16.2 us
  between operations: 14.1 us -> 0.91 us
  other arithmetic: 6.79 us -> 0 us
    all_to_all x1 -> x0, waiting for transfers between devices: 93.7 us -> none  [on_device(): lax.all_to_all(low, 'dp', split_axis=2, concat_axis=1, tiled=True)]
    ppermute x0 -> x18, starting transfers between devices: none -> 43.8 us  [send(): return lax.ppermute(array, 'dp', shift(*delta))]
    unnamed x2 -> x0, waiting for transfers between devices: 41 us -> none
    ppermute x0 -> x18, waiting for transfers between devices: none -> 36.8 us  [send(): return lax.ppermute(array, 'dp', shift(*delta))]
    unnamed x12 -> x6, local copies, waits for them, and re-layouts: 32.3 us -> 0.01 us
    all_to_all x0 -> x2, blocking collectives: none -> 29 us  [exchange(): lax.all_to_all(array, 'tensor', split_axis=0, concat_axis=0, tiled=True)]
    all_to_all x1 -> x0, local copies, waits for them, and re-layouts: 18.5 us -> none  [on_device(): lax.all_to_all(low, 'dp', split_axis=2, concat_axis=1, tiled=True)]
    convert_element_type x1 -> x0, local copies, waits for them, and re-layouts: 17.8 us -> none  [on_device(): low = master.astype(jnp.bfloat16)]
  transfers between devices with their start and end apart: 2 -> 18, of which waited for: 2 -> 3; matrix products, arithmetic and copies ran while one was open for 0% -> 0% of each run, Pallas kernels for 0% -> 9%
where the time goes in v3:
time: 128 us; the launch traced here: 127 us
  starting transfers between devices  43.8 us (34%)
  waiting for transfers between devices  36.8 us (29%)
  blocking collectives  29 us (23%)
  Pallas kernels  16.2 us (13%)
    ppermute x18, starting transfers between devices, send(): return lax.ppermute(array, 'dp', shift(*delta))  43.8 us
    ppermute x18, waiting for transfers between devices, send(): return lax.ppermute(array, 'dp', shift(*delta))  36.8 us
    all_to_all x2, blocking collectives, exchange(): lax.all_to_all(array, 'tensor', split_axis=0, concat_axis=0, tiled=True)  29 us
    pallas_call x4, Pallas kernels, pack(): pl.pallas_call(functools.partial(pack_kernel, blocks, copies, len(shapes)...  9.49 us
    pallas_call x2, Pallas kernels, regroup(): pl.pallas_call(functools.partial(regroup_kernel, chips, before is not Non...  4.1 us
  transfers between devices with their start and end apart: 18, of which 3 were waited for; matrix products, arithmetic and copies ran while one was open for 0% of the time, Pallas kernels for 9%

profile of v3, /device:TPU:4, one launch (start us, length us, event | category | flops | bytes accessed | tf_op | source)
XLA Modules:
  0.0 126.7 jit_solution(9483858190554678155)
XLA Ops:
  0.6 2.2 %shard_map.50 = bf16[14,2,64,512]{3,2,1,0:T(8,128)(2,1)S(1)} custom-call(f32[2,64,16384]{2,1,0:T(8,128)} %refs_0_.7), custom_call_target="tpu_custom_call" | custom-call | bytes 5505024 | tf_op jit(solution)/shard_map/pallas_call | solution.py:146
  2.8 0.1 collective-permute-start
  2.9 1.3 %shard_map.52 = (bf16[128,512]{1,0:T(8,128)(2,1)S(1)}, bf16[128,512]{1,0:T(8,128)(2,1)S(1)}, bf16[128,512]{1,0:T(8,128)(2,1)S(1)}, bf16[128,512]{1,0:T(8,128)(2,1)S(1)}) custom-call(f32[2,64,16384]{2,1,0:T(8,128)} %refs_0_.7), custom_call_target="tpu_custom_call" | custom-call | bytes 1572864 | tf_op jit(solution)/shard_map/pallas_call | solution.py:146
  4.2 7.3 %collective-permute-start.5 = (bf16[128,512]{1,0:T(8,128)(2,1)S(1)}, bf16[128,512]{1,0:T(8,128)(2,1)S(1)}, u32[]{:S(2)}, u32[]{:S(2)}) collective-permute-start(bf16[128,512]{1,0:T(8,128)(2,1)S(1)} %get-tuple-element.35), channel_id=1, source_target_pairs={{0,64},{8,72},{16,80},{24,88},{32,96},{40,104},{48,112},{56,120},{... | collective-permute-start | bytes 393224 | tf_op jit(solution)/shard_map/ppermute | solution.py:27
  11.4 0.0 copy-start.1
  11.5 0.0 copy-start.2
  11.5 0.2 collective-permute-start.6
  11.6 0.0 collective-permute-done.refs_1_
  11.6 0.0 copy-start
  11.7 1.9 %shard_map.53 = (bf16[256,512]{1,0:T(8,128)(2,1)S(1)}, bf16[256,512]{1,0:T(8,128)(2,1)S(1)}, bf16[256,512]{1,0:T(8,128)(2,1)S(1)}, bf16[256,512]{1,0:T(8,128)(2,1)S(1)}) custom-call(f32[2,64,16384]{2,1,0:T(8,128)} %refs_0_.7, bf16[14,2,64,512]{3,2,1,0:T(8,128)(2,1)S(1)} %collective-permute-done.refs_1_), custom_call_target="tpu_custom_call" | custom-call | bytes 2621440 | tf_op jit(solution)/shard_map/pallas_call | solution.py:146
  13.6 0.0 copy-done
  13.6 3.0 %collective-permute-start.9 = (bf16[256,512]{1,0:T(8,128)(2,1)S(1)}, bf16[256,512]{1,0:T(8,128)(2,1)S(1)}, u32[]{:S(2)}, u32[]{:S(2)}) collective-permute-start(bf16[256,512]{1,0:T(8,128)(2,1)S(1)} %get-tuple-element.39), channel_id=1, source_target_pairs={{0,176},{8,184},{16,192},{24,200},{32,208},{40,216},{48,224},{56,2... | collective-permute-start | bytes 786440 | tf_op jit(solution)/shard_map/ppermute | solution.py:27
  16.6 4.5 %collective-permute-start.10 = (bf16[256,512]{1,0:T(8,128)(2,1)S(1)}, bf16[256,512]{1,0:T(8,128)(2,1)S(1)}, u32[]{:S(2)}, u32[]{:S(2)}) collective-permute-start(bf16[256,512]{1,0:T(8,128)(2,1)S(1)} %get-tuple-element.40), channel_id=1, source_target_pairs={{0,208},{8,216},{16,224},{24,232},{32,240},{40,248},{48,128},{56,1... | collective-permute-start | bytes 786440 | tf_op jit(solution)/shard_map/ppermute | solution.py:27
  21.1 1.8 %collective-permute-start.11 = (bf16[256,512]{1,0:T(8,128)(2,1)S(1)}, bf16[256,512]{1,0:T(8,128)(2,1)S(1)}, u32[]{:S(2)}, u32[]{:S(2)}) collective-permute-start(bf16[256,512]{1,0:T(8,128)(2,1)S(1)} %get-tuple-element.41), channel_id=1, source_target_pairs={{0,48},{8,56},{16,64},{24,72},{32,80},{40,88},{48,96},{56,104},{64... | collective-permute-start | bytes 786440 | tf_op jit(solution)/shard_map/ppermute | solution.py:27
  22.9 0.0 collective-permute-done.5.refs_3_
  22.9 4.4 %collective-permute-start.7 = (bf16[128,512]{1,0:T(8,128)(2,1)S(1)}, bf16[128,512]{1,0:T(8,128)(2,1)S(1)}, u32[]{:S(2)}, u32[]{:S(2)}) collective-permute-start(bf16[128,512]{1,0:T(8,128)(2,1)S(1)} %get-tuple-element.37), channel_id=1, source_target_pairs={{0,192},{8,200},{16,208},{24,216},{32,224},{40,232},{48,240},{56,2... | collective-permute-start | bytes 393224 | tf_op jit(solution)/shard_map/ppermute | solution.py:27
  27.3 0.0 collective-permute-done.6.refs_4_
  27.3 2.7 %collective-permute-start.8 = (bf16[128,512]{1,0:T(8,128)(2,1)S(1)}, bf16[128,512]{1,0:T(8,128)(2,1)S(1)}, u32[]{:S(2)}, u32[]{:S(2)}) collective-permute-start(bf16[128,512]{1,0:T(8,128)(2,1)S(1)} %get-tuple-element.38), channel_id=1, source_target_pairs={{0,200},{8,192},{16,216},{24,208},{32,232},{40,224},{48,248},{56,2... | collective-permute-start | bytes 393224 | tf_op jit(solution)/shard_map/ppermute | solution.py:27
  30.0 0.0 copy-done.1
  30.0 0.0 copy-done.2
  30.0 4.1 %shard_map.51 = (bf16[256,512]{1,0:T(8,128)(2,1)S(1)}, bf16[256,512]{1,0:T(8,128)(2,1)S(1)}, bf16[256,512]{1,0:T(8,128)(2,1)S(1)}, bf16[256,512]{1,0:T(8,128)(2,...) custom-call(f32[2,64,16384]{2,1,0:T(8,128)} %refs_0_.7, ...), custom_call_target="tpu_custom_call" | custom-call | flops 10485760 | bytes 6553600 | tf_op jit(solution)/shard_map/pallas_call | solution.py:146
  34.2 31.7 %collective-permute-done.7.refs_5_ = bf16[128,512]{1,0:T(8,128)(2,1)S(1)} collective-permute-done((bf16[128,512]{1,0:T(8,128)(2,1)S(1)}, bf16[128,512]{1,0:T(8,128)(2,1)S(1)}, u32[]{:S(2)}, u32[]{:S(2)}) %collective-permute-start.7) | collective-permute-done | bytes 131104 | tf_op jit(solution)/shard_map/ppermute | solution.py:27
  65.9 0.0 collective-permute-start.12
  65.9 4.4 %collective-permute-done.8.refs_6_ = bf16[128,512]{1,0:T(8,128)(2,1)S(1)} collective-permute-done((bf16[128,512]{1,0:T(8,128)(2,1)S(1)}, bf16[128,512]{1,0:T(8,128)(2,1)S(1)}, u32[]{:S(2)}, u32[]{:S(2)}) %collective-permute-start.8) | collective-permute-done | bytes 131104 | tf_op jit(solution)/shard_map/ppermute | solution.py:27
  70.4 1.4 %collective-permute-start.1 = (bf16[256,512]{1,0:T(8,128)(2,1)S(1)}, bf16[256,512]{1,0:T(8,128)(2,1)S(1)}, u32[]{:S(2)}, u32[]{:S(2)}) collective-permute-start(bf16[256,512]{1,0:T(8,128)(2,1)S(1)} %get-tuple-element.30), channel_id=1, source_target_pairs={{0,160},{8,168},{16,176},{24,184},{32,192},{40,200},{48,208},{56,2... | collective-permute-start | bytes 786440 | tf_op jit(solution)/shard_map/ppermute | solution.py:27
  71.8 0.0 collective-permute-done.9.refs_7_
  71.8 5.1 %collective-permute-start.2 = (bf16[256,512]{1,0:T(8,128)(2,1)S(1)}, bf16[256,512]{1,0:T(8,128)(2,1)S(1)}, u32[]{:S(2)}, u32[]{:S(2)}) collective-permute-start(bf16[256,512]{1,0:T(8,128)(2,1)S(1)} %get-tuple-element.31), channel_id=1, source_target_pairs={{0,224},{8,232},{16,240},{24,248},{32,128},{40,136},{48,144},{56,1... | collective-permute-start | bytes 786440 | tf_op jit(solution)/shard_map/ppermute | solution.py:27
  76.9 0.0 collective-permute-done.10.refs_8_
  76.9 0.0 collective-permute-start.3
  76.9 0.0 collective-permute-done.11.refs_9_
  76.9 4.1 %collective-permute-start.4 = (bf16[256,512]{1,0:T(8,128)(2,1)S(1)}, bf16[256,512]{1,0:T(8,128)(2,1)S(1)}, u32[]{:S(2)}, u32[]{:S(2)}) collective-permute-start(bf16[256,512]{1,0:T(8,128)(2,1)S(1)} %get-tuple-element.33), channel_id=1, source_target_pairs={{0,96},{8,104},{16,112},{24,120},{32,0},{40,8},{48,16},{56,24},{64... | collective-permute-start | bytes 786440 | tf_op jit(solution)/shard_map/ppermute | solution.py:27
  81.0 18.6 %all_to_all.10.parts_ref = f32[8,5,8,128]{3,2,1,0:T(8,128)S(1)} all-to-all(f32[8,5,8,128]{3,2,1,0:T(8,128)S(1)} %get-tuple-element.46), channel_id=1, replica_groups=mesh['dp'=32,'tensor'=8] {'tensor'}, dimensions={0} | all-to-all | bytes 327680 | tf_op jit(solution)/shard_map/all_to_all | solution.py:31
  99.6 0.2 attach.1
  99.8 0.0 collective-permute-done.12.refs_10_
  99.8 0.9 collective-permute-start.13
  100.7 0.0 collective-permute-done.1.refs_2_
  100.7 0.0 collective-permute-start.14
  100.7 0.0 collective-permute-done.2.refs_3_
  100.8 5.6 %collective-permute-start.15 = (bf16[264,512]{1,0:T(8,128)(2,1)S(1)}, bf16[264,512]{1,0:T(8,128)(2,1)S(1)}, u32[]{:S(2)}, u32[]{:S(2)}) collective-permute-start(bf16[264,512]{1,0:T(8,128)(2,1)S(1)} %get-tuple-element.54), channel_id=1, source_target_pairs={{0,240},{8,248},{16,128},{24,136},{32,144},{40,152},{48,160},{56,1... | collective-permute-start | bytes 811016 | tf_op jit(solution)/shard_map/ppermute | solution.py:27
  106.4 0.0 collective-permute-done.3.refs_4_
  106.4 0.0 collective-permute-start.16
  106.4 0.6 collective-permute-done.4.refs_5_
  107.0 2.6 %collective-permute-start.17 = (bf16[264,512]{1,0:T(8,128)(2,1)S(1)}, bf16[264,512]{1,0:T(8,128)(2,1)S(1)}, u32[]{:S(2)}, u32[]{:S(2)}) collective-permute-start(bf16[264,512]{1,0:T(8,128)(2,1)S(1)} %get-tuple-element.56), channel_id=1, source_target_pairs={{0,112},{8,120},{16,0},{24,8},{32,16},{40,24},{48,32},{56,40},{64,... | collective-permute-start | bytes 811016 | tf_op jit(solution)/shard_map/ppermute | solution.py:27
  109.6 2.4 %shard_map.54 = (bf16[2,2048,512]{2,1,0:T(8,128)(2,1)}, f32[2,8,512]{2,1,0:T(8,128)S(1)}) custom-call(s32[16]{0:T(128)S(1)} %bitcast.2, s32[8,2048]{1,0:T(8,128)S(1)} %copy-done.1, bf16[256,512]{1,0:T(8,128)(2,1)S(1)} %get-tuple-element.34.refs_2_, bf16[128,512]{1,0:T(8,128)(2,1)S(1)} %collective-permute-done.5.refs_3_, ...), custom_call_target="tpu_custom_call" | custom-call | flops 14680064 | bytes 3670016 | tf_op jit(solution)/shard_map/pallas_call | solution.py:232
  112.0 1.7 %shard_map.55 = (bf16[2,2048,512]{2,1,0:T(8,128)(2,1)}, f32[8,8,128]{2,1,0:T(8,128)S(1)}) custom-call(s32[16]{0:T(128)S(1)} %bitcast.3, s32[8,2048]{1,0:T(8,128)S(1)} %copy-done.1, bf16[256,512]{1,0:T(8,128)(2,1)S(1)} %collective-permute-done.1.refs_2_, bf16[256,512]{1,0:T(8,128)(2,1)S(1)} %collective-permute-done.2.refs_3_, ...), custom_call_target="tpu_custom_call", output_to_operand_aliasing={{0}: (7, {})} | custom-call | flops 8388608 | bytes 2097152 | tf_op jit(solution)/shard_map/pallas_call | solution.py:232
  113.8 10.4 %all_to_all.11.refs_1_ = f32[8,8,128]{2,1,0:T(8,128)S(1)} all-to-all(f32[8,8,128]{2,1,0:T(8,128)S(1)} %get-tuple-element.45), channel_id=1, replica_groups=mesh['dp'=32,'tensor'=8] {'tensor'}, dimensions={0} | all-to-all | bytes 65536 | tf_op jit(solution)/shard_map/all_to_all | solution.py:31
  124.1 0.0 collective-permute-done.13.refs_2_
  124.1 0.0 collective-permute-done.14.refs_3_
  124.1 0.0 collective-permute-done.15.refs_4_
  124.1 0.0 collective-permute-done.16.refs_5_
  124.2 0.0 collective-permute-done.17.refs_6_
  124.2 2.4 %finish.1 = (bf16[2,2048,512]{2,1,0:T(8,128)(2,1)}, f32[2,8,64]{2,1,0:T(8,128)}) custom-call(s32[16]{0:T(128)S(1)} %bitcast.4, f32[8,8,128]{2,1,0:T(8,128)S(1)} %all_to_all.11.refs_1_, bf16[264,512]{1,0:T(8,128)(2,1)S(1)} %collective-permute-done.13.refs_2_, bf16[264,512]{1,0:T(8,128)(2,1)S(1)} %collective-permute-done.14.refs_3_, ...), custom_call_target="tpu_custom_call", output_to_operand_aliasing={{0}: (7, {})} | custom-call | tf_op jit(solution)/shard_map/finish/pallas_call | solution.py:316
Async XLA Ops:
  2.8 8.9 %collective-permute-start = (bf16[14,2,64,512]{3,2,1,0:T(8,128)(2,1)S(1)}, bf16[14,2,64,512]{3,2,1,0:T(8,128)(2,1)S(1)}, u32[]{:S(2)}, u32[]{:S(2)}) collective-permute-start(bf16[14,2,64,512]{3,2,1,0:T(8,128)(2,1)S(1)} %shard_map.50), channel_id=1, source_target_pairs={{0,8},{8,0},{16,24},{24,16},{32,40},{40,32},{48,56},{56,48},{64,72... | collective-permute-start | bytes 5505032 | tf_op jit(solution)/shard_map/ppermute | solution.py:27
  4.2 18.7 %collective-permute-start.5 = (bf16[128,512]{1,0:T(8,128)(2,1)S(1)}, bf16[128,512]{1,0:T(8,128)(2,1)S(1)}, u32[]{:S(2)}, u32[]{:S(2)}) collective-permute-start(bf16[128,512]{1,0:T(8,128)(2,1)S(1)} %get-tuple-element.35), channel_id=1, source_target_pairs={{0,64},{8,72},{16,80},{24,88},{32,96},{40,104},{48,112},{56,120},{... | collective-permute-start | bytes 393224 | tf_op jit(solution)/shard_map/ppermute | solution.py:27
  11.4 18.6 %copy-start.1 = (s32[8,2048]{1,0:T(8,128)S(1)}, s32[8,2048]{1,0:T(8,128)}, u32[]{:S(2)}) copy-start(s32[8,2048]{1,0:T(8,128)} %refs_1_.3) | copy-start | bytes 196612
  11.5 18.6 %copy-start.2 = (s32[1,16]{1,0:T(1,128)S(1)}, s32[1,16]{1,0:T(1,128)}, u32[]{:S(2)}) copy-start(s32[1,16]{1,0:T(1,128)} %param.4) | copy-start | bytes 196
  11.5 15.8 %collective-permute-start.6 = (bf16[128,512]{1,0:T(8,128)(2,1)S(1)}, bf16[128,512]{1,0:T(8,128)(2,1)S(1)}, u32[]{:S(2)}, u32[]{:S(2)}) collective-permute-start(bf16[128,512]{1,0:T(8,128)(2,1)S(1)} %get-tuple-element.36), channel_id=1, source_target_pairs={{0,72},{8,64},{16,88},{24,80},{32,104},{40,96},{48,120},{56,112},{... | collective-permute-start | bytes 393224 | tf_op jit(solution)/shard_map/ppermute | solution.py:27
  11.6 1.9 %copy-start = (bf16[14,2,64,512]{3,2,1,0:T(8,128)(2,1)}, bf16[14,2,64,512]{3,2,1,0:T(8,128)(2,1)S(1)}, u32[]{:S(2)}) copy-start(bf16[14,2,64,512]{3,2,1,0:T(8,128)(2,1)S(1)} %collective-permute-done.refs_1_) | copy-start | bytes 5505028
  13.6 58.2 %collective-permute-start.9 = (bf16[256,512]{1,0:T(8,128)(2,1)S(1)}, bf16[256,512]{1,0:T(8,128)(2,1)S(1)}, u32[]{:S(2)}, u32[]{:S(2)}) collective-permute-start(bf16[256,512]{1,0:T(8,128)(2,1)S(1)} %get-tuple-element.39), channel_id=1, source_target_pairs={{0,176},{8,184},{16,192},{24,200},{32,208},{40,216},{48,224},{56,2... | collective-permute-start | bytes 786440 | tf_op jit(solution)/shard_map/ppermute | solution.py:27
  16.6 60.3 %collective-permute-start.10 = (bf16[256,512]{1,0:T(8,128)(2,1)S(1)}, bf16[256,512]{1,0:T(8,128)(2,1)S(1)}, u32[]{:S(2)}, u32[]{:S(2)}) collective-permute-start(bf16[256,512]{1,0:T(8,128)(2,1)S(1)} %get-tuple-element.40), channel_id=1, source_target_pairs={{0,208},{8,216},{16,224},{24,232},{32,240},{40,248},{48,128},{56,1... | collective-permute-start | bytes 786440 | tf_op jit(solution)/shard_map/ppermute | solution.py:27
  21.1 55.8 %collective-permute-start.11 = (bf16[256,512]{1,0:T(8,128)(2,1)S(1)}, bf16[256,512]{1,0:T(8,128)(2,1)S(1)}, u32[]{:S(2)}, u32[]{:S(2)}) collective-permute-start(bf16[256,512]{1,0:T(8,128)(2,1)S(1)} %get-tuple-element.41), channel_id=1, source_target_pairs={{0,48},{8,56},{16,64},{24,72},{32,80},{40,88},{48,96},{56,104},{64... | collective-permute-start | bytes 786440 | tf_op jit(solution)/shard_map/ppermute | solution.py:27
  22.9 43.0 %collective-permute-start.7 = (bf16[128,512]{1,0:T(8,128)(2,1)S(1)}, bf16[128,512]{1,0:T(8,128)(2,1)S(1)}, u32[]{:S(2)}, u32[]{:S(2)}) collective-permute-start(bf16[128,512]{1,0:T(8,128)(2,1)S(1)} %get-tuple-element.37), channel_id=1, source_target_pairs={{0,192},{8,200},{16,208},{24,216},{32,224},{40,232},{48,240},{56,2... | collective-permute-start | bytes 393224 | tf_op jit(solution)/shard_map/ppermute | solution.py:27
  27.3 43.0 %collective-permute-start.8 = (bf16[128,512]{1,0:T(8,128)(2,1)S(1)}, bf16[128,512]{1,0:T(8,128)(2,1)S(1)}, u32[]{:S(2)}, u32[]{:S(2)}) collective-permute-start(bf16[128,512]{1,0:T(8,128)(2,1)S(1)} %get-tuple-element.38), channel_id=1, source_target_pairs={{0,200},{8,192},{16,216},{24,208},{32,232},{40,224},{48,248},{56,2... | collective-permute-start | bytes 393224 | tf_op jit(solution)/shard_map/ppermute | solution.py:27
  65.9 33.9 %collective-permute-start.12 = (bf16[256,512]{1,0:T(8,128)(2,1)S(1)}, bf16[256,512]{1,0:T(8,128)(2,1)S(1)}, u32[]{:S(2)}, u32[]{:S(2)}) collective-permute-start(bf16[256,512]{1,0:T(8,128)(2,1)S(1)} %get-tuple-element.42), channel_id=1, source_target_pairs={{0,80},{8,88},{16,96},{24,104},{32,112},{40,120},{48,0},{56,8},{64... | collective-permute-start | bytes 786440 | tf_op jit(solution)/shard_map/ppermute | solution.py:27
  70.4 30.4 %collective-permute-start.1 = (bf16[256,512]{1,0:T(8,128)(2,1)S(1)}, bf16[256,512]{1,0:T(8,128)(2,1)S(1)}, u32[]{:S(2)}, u32[]{:S(2)}) collective-permute-start(bf16[256,512]{1,0:T(8,128)(2,1)S(1)} %get-tuple-element.30), channel_id=1, source_target_pairs={{0,160},{8,168},{16,176},{24,184},{32,192},{40,200},{48,208},{56,2... | collective-permute-start | bytes 786440 | tf_op jit(solution)/shard_map/ppermute | solution.py:27
  71.8 29.0 %collective-permute-start.2 = (bf16[256,512]{1,0:T(8,128)(2,1)S(1)}, bf16[256,512]{1,0:T(8,128)(2,1)S(1)}, u32[]{:S(2)}, u32[]{:S(2)}) collective-permute-start(bf16[256,512]{1,0:T(8,128)(2,1)S(1)} %get-tuple-element.31), channel_id=1, source_target_pairs={{0,224},{8,232},{16,240},{24,248},{32,128},{40,136},{48,144},{56,1... | collective-permute-start | bytes 786440 | tf_op jit(solution)/shard_map/ppermute | solution.py:27
  76.9 29.5 %collective-permute-start.3 = (bf16[256,512]{1,0:T(8,128)(2,1)S(1)}, bf16[256,512]{1,0:T(8,128)(2,1)S(1)}, u32[]{:S(2)}, u32[]{:S(2)}) collective-permute-start(bf16[256,512]{1,0:T(8,128)(2,1)S(1)} %get-tuple-element.32), channel_id=1, source_target_pairs={{0,32},{8,40},{16,48},{24,56},{32,64},{40,72},{48,80},{56,88},{64,... | collective-permute-start | bytes 786440 | tf_op jit(solution)/shard_map/ppermute | solution.py:27
  76.9 30.1 %collective-permute-start.4 = (bf16[256,512]{1,0:T(8,128)(2,1)S(1)}, bf16[256,512]{1,0:T(8,128)(2,1)S(1)}, u32[]{:S(2)}, u32[]{:S(2)}) collective-permute-start(bf16[256,512]{1,0:T(8,128)(2,1)S(1)} %get-tuple-element.33), channel_id=1, source_target_pairs={{0,96},{8,104},{16,112},{24,120},{32,0},{40,8},{48,16},{56,24},{64... | collective-permute-start | bytes 786440 | tf_op jit(solution)/shard_map/ppermute | solution.py:27
  99.8 24.3 %collective-permute-start.13 = (bf16[264,512]{1,0:T(8,128)(2,1)S(1)}, bf16[264,512]{1,0:T(8,128)(2,1)S(1)}, u32[]{:S(2)}, u32[]{:S(2)}) collective-permute-start(bf16[264,512]{1,0:T(8,128)(2,1)S(1)} %get-tuple-element.52), channel_id=1, source_target_pairs={{0,128},{8,136},{16,144},{24,152},{32,160},{40,168},{48,176},{56,1... | collective-permute-start | bytes 811016 | tf_op jit(solution)/shard_map/ppermute | solution.py:27
  100.7 23.4 %collective-permute-start.14 = (bf16[264,512]{1,0:T(8,128)(2,1)S(1)}, bf16[264,512]{1,0:T(8,128)(2,1)S(1)}, u32[]{:S(2)}, u32[]{:S(2)}) collective-permute-start(bf16[264,512]{1,0:T(8,128)(2,1)S(1)} %get-tuple-element.53), channel_id=1, source_target_pairs={{0,144},{8,152},{16,160},{24,168},{32,176},{40,184},{48,192},{56,2... | collective-permute-start | bytes 811016 | tf_op jit(solution)/shard_map/ppermute | solution.py:27
  100.8 23.4 %collective-permute-start.15 = (bf16[264,512]{1,0:T(8,128)(2,1)S(1)}, bf16[264,512]{1,0:T(8,128)(2,1)S(1)}, u32[]{:S(2)}, u32[]{:S(2)}) collective-permute-start(bf16[264,512]{1,0:T(8,128)(2,1)S(1)} %get-tuple-element.54), channel_id=1, source_target_pairs={{0,240},{8,248},{16,128},{24,136},{32,144},{40,152},{48,160},{56,1... | collective-permute-start | bytes 811016 | tf_op jit(solution)/shard_map/ppermute | solution.py:27
  106.4 17.8 %collective-permute-start.16 = (bf16[264,512]{1,0:T(8,128)(2,1)S(1)}, bf16[264,512]{1,0:T(8,128)(2,1)S(1)}, u32[]{:S(2)}, u32[]{:S(2)}) collective-permute-start(bf16[264,512]{1,0:T(8,128)(2,1)S(1)} %get-tuple-element.55), channel_id=1, source_target_pairs={{0,16},{8,24},{16,32},{24,40},{32,48},{40,56},{48,64},{56,72},{64,... | collective-permute-start | bytes 811016 | tf_op jit(solution)/shard_map/ppermute | solution.py:27
  107.0 17.1 %collective-permute-start.17 = (bf16[264,512]{1,0:T(8,128)(2,1)S(1)}, bf16[264,512]{1,0:T(8,128)(2,1)S(1)}, u32[]{:S(2)}, u32[]{:S(2)}) collective-permute-start(bf16[264,512]{1,0:T(8,128)(2,1)S(1)} %get-tuple-element.56), channel_id=1, source_target_pairs={{0,112},{8,120},{16,0},{24,8},{32,16},{40,24},{48,32},{56,40},{64,... | collective-permute-start | bytes 811016 | tf_op jit(solution)/shard_map/ppermute | solution.py:27
